TPU v7x, 256 devices: a whole 4x4x8 slice. The times are simulated.
256 devices in a mesh: row: 8 (over z), col: 32 (over y, x, core).
Axes of the slice: x: 4, y: 4, z: 8, core: 2. Of those that a mesh axis runs over, the one named last changes fastest.
Arguments:
- tiles: bfloat16 [8, 32, 16, 576, 576], P('row', 'col'), may hold values from -0.0625 to 0.0625
- diag_tiles: bfloat16 [256, 576, 576], P(('row', 'col')), as said below
- probes: float32 [256, 64, 576], P(('row', 'col'))
- rows_list: int32 [8, 32, 16], P('row', 'col'), may hold values from 0 to 31, as said below
- cols_list: int32 [8, 32, 16], P('row', 'col'), may hold values from 0 to 7, as said below
- counts: int32 [8, 32], P('row', 'col'), may hold values from 0 to 16, as said below
Outputs:
- solution: float32 [256, 64, 576], P(('row', 'col'))
- residual: float32 [256, 64, 576], P(('row', 'col'))
Inputs may be any that keep to these rules, and one draw needn't show every extreme that they name: `rows_list`: slots past a device's count hold 0; a held slot lies strictly below the diagonal. `cols_list`: slots past a device's count hold 0. `counts`: the busiest device holds 16 tiles. `diag_tiles`: each diagonal tile is symmetric positive definite: its diagonal entries are at least 4.4 and its off-diagonal part has spectral radius below about 1.
All inputs are finite; a program needn't handle non-finite values.
Results may differ from a plain program's by a relative error of at most 0.039.
Values may be sent and summed in bfloat16 or wider, within the bound.
A program may use at most 128 MiB of HBM per device.

v0:
```python
import jax
import jax.numpy as jnp
from jax import lax
from jax.sharding import PartitionSpec as P

ITERS = 2


def gram_local(left, right):
    return jnp.einsum("tpb,tqb->pq", left, right, precision=lax.Precision.HIGHEST)


def combine(coef, block):
    return jnp.einsum("pq,tpb->tqb", coef, block, precision=lax.Precision.HIGHEST)


def solve_with(matrix, rhs):
    factor = jnp.linalg.cholesky(matrix)
    middle = lax.linalg.triangular_solve(factor, rhs, left_side=True, lower=True, transpose_a=False)
    return lax.linalg.triangular_solve(factor, middle, left_side=True, lower=True, transpose_a=True)


def curvature_sum(direction, image):
    return lax.psum(gram_local(direction, image), ("row", "col"))


def apply_operator(rounded, tiles, diag_tiles, rows_list, cols_list, counts):
    row_probe = lax.all_gather(rounded, "col", axis=0, tiled=True)
    col_probe = lax.all_gather(rounded, "row", axis=0, tiled=True)
    width_p = rounded.shape[1]
    width_b = rounded.shape[2]
    own = lax.dot_general(
        rounded[0], diag_tiles[0], (((1,), (1,)), ((), ())), preferred_element_type=jnp.float32
    )

    def turn(slot, carry):
        acc_row, acc_col = carry
        local = rows_list[0, 0, slot]
        source = cols_list[0, 0, slot]
        block = tiles[0, 0, slot]
        far = col_probe[source]
        near = row_probe[local]
        fwd = lax.dot_general(
            far, block, (((1,), (1,)), ((), ())), preferred_element_type=jnp.float32
        )
        bwd = jnp.dot(near, block, preferred_element_type=jnp.float32)
        return (acc_row.at[local].add(fwd), acc_col.at[source].add(bwd))

    start = (
        jnp.zeros((row_probe.shape[0], width_p, width_b), jnp.float32),
        jnp.zeros((col_probe.shape[0], width_p, width_b), jnp.float32),
    )
    acc_row, acc_col = lax.fori_loop(0, counts[0, 0], turn, start)
    forward = lax.psum_scatter(
        acc_row.astype(jnp.bfloat16), "col", scatter_dimension=0, tiled=True
    ).astype(jnp.float32)
    mirrored = lax.psum_scatter(
        acc_col.astype(jnp.bfloat16), "row", scatter_dimension=0, tiled=True
    ).astype(jnp.float32)
    return forward + mirrored + own[None]


def body(tiles, diag_tiles, probes, rows_list, cols_list, counts):
    solution = jnp.zeros(probes.shape, jnp.float32)
    residual = probes
    direction = probes
    norm_now = lax.psum(gram_local(residual, residual), ("row", "col"))
    for step in range(ITERS):
        image = apply_operator(
            direction.astype(jnp.bfloat16), tiles, diag_tiles, rows_list, cols_list, counts
        )
        final = step + 1 == ITERS
        curv = curvature_sum(direction, image)
        alpha = solve_with(curv, norm_now)
        solution = solution + combine(alpha, direction)
        residual = residual - combine(alpha, image)
        if not final:
            norm_next = lax.psum(gram_local(residual, residual), ("row", "col"))
            beta = solve_with(norm_now, norm_next)
            direction = residual + combine(beta, direction)
            norm_now = norm_next
    return (solution, residual)


def solution(mesh):
    placed = (
        P("row", "col", None, None, None),
        P(("row", "col"), None, None),
        P(("row", "col"), None, None),
        P("row", "col", None),
        P("row", "col", None),
        P("row", "col"),
    )
    return jax.shard_map(
        body,
        mesh=mesh,
        in_specs=placed,
        out_specs=(P(("row", "col"), None, None), P(("row", "col"), None, None)),
        check_vma=False,
    )
```

profile of v0, /device:TPU:8, one launch (start us, length us, event | category | flops | bytes accessed | tf_op | source)
XLA Modules:
  0.0 989.4 jit_solution(8945101122827908853)
XLA Ops:
  7.3 1.6 convert_element_type.30
  9.0 29.6 %all_gather.12 = bf16[8,64,576]{2,1,0:T(8,128)(2,1)S(1)} all-gather(bf16[1,64,576]{2,1,0:T(8,128)(2,1)} %convert_element_type.30), channel_id=1, replica_groups=mesh['row'=8,'col'=32] {'row'}, dimensions={0}, use_global_device_ids=true | all-gather | bytes 663552 | tf_op jit(solution)/shard_map/all_gather | solution.py:29
  38.6 24.7 %all-gather.3.cloned.1.call-done = bf16[32,64,576]{2,1,0:T(8,128)(2,1)} async-done(((bf16[1,64,576]{2,1,0:T(8,128)(2,1)}), bf16[32,64,576]{2,1,0:T(8,128)(2,1)}) %all-gather.3.cloned.1.call-update) | async-done | bytes 2359312 | tf_op jit(solution)/shard_map/all_gather | solution.py:28
  63.3 2.9 broadcast.110.clone
  66.3 11.5 %while.28 = (s32[]{:T(128)}, f32[32,64,576]{2,1,0:T(8,128)}, f32[8,64,576]{2,1,0:T(8,128)S(1)}, s32[]{:T(128)}, s32[1,1,16]{2,1,0:T(1,128)S(1)}, /*index=5*/s32[...) while((s32[]{:T(128)}, f32[32,64,576]{2,1,0:T(8,128)}, ...), condition=%wide.region_3.4_spmd, body=%wide.region_0.3_spmd.sunk | while | flops 85082160 | bytes 2297161 | solution.py:53
  71.8 2.7 fusion.104
  75.2 2.0 fusion.105
  78.9 4.4 convert_element_type.31
  83.7 193.1 %reduce-scatter.7.cloned.1.call-done = bf16[1,64,576]{2,1,0:T(8,128)(2,1)} async-done(((bf16[8,64,576]{2,1,0:T(8,128)(2,1)}), bf16[1,64,576]{2,1,0:T(8,128)(2,1)}) %reduce-scatter.7.cloned.1.call-update) | async-done | bytes 73744 | tf_op jit(solution)/shard_map/reduce_scatter | solution.py:57
  276.8 89.2 %reduce-scatter.5.cloned.1.call-done = bf16[1,64,576]{2,1,0:T(8,128)(2,1)} async-done(((bf16[32,64,576]{2,1,0:T(8,128)(2,1)}), bf16[1,64,576]{2,1,0:T(8,128)(2,1)}) %reduce-scatter.5.cloned.1.call-update) | async-done | bytes 73744 | tf_op jit(solution)/shard_map/reduce_scatter | solution.py:54
  366.0 1.3 fusion.37
  367.6 74.1 %all-reduce = (f32[64,64]{0,1:T(8,128)S(1)}, f32[64,64]{0,1:T(8,128)S(1)}) all-reduce(f32[64,64]{0,1:T(8,128)S(1)} %fusion.49, f32[64,64]{0,1:T(8,128)S(1)} %convolution_bitcast_fusion.10), channel_id=1, replica_groups=mesh['row'=8,'col'=32] {'row','col'}, use_global_device_ids=true, to_apply=%region_9.11 | all-reduce | flops 8192 | bytes 65536 | tf_op jit(solution)/shard_map/psum | solution.py:67
  441.9 5.8 cholesky.70
  449.1 4.9 custom-call.15
  453.9 5.9 cholesky.59
  461.2 4.9 custom-call.13
  467.1 74.6 %psum.30 = f32[64,64]{1,0:T(8,128)S(1)} all-reduce(f32[64,64]{1,0:T(8,128)S(1)} %fusion.45), channel_id=1, replica_groups=mesh['row'=8,'col'=32] {'row','col'}, use_global_device_ids=true, to_apply=%region_10.14 | all-reduce | flops 4096 | bytes 32768 | tf_op jit(solution)/shard_map/psum | solution.py:78
  543.2 26.1 %all_gather.14 = bf16[8,64,576]{2,1,0:T(8,128)(2,1)S(1)} all-gather(bf16[1,64,576]{2,1,0:T(8,128)(2,1)} %get-tuple-element.197), channel_id=1, replica_groups=mesh['row'=8,'col'=32] {'row'}, dimensions={0}, use_global_device_ids=true | all-gather | bytes 663552 | tf_op jit(solution)/shard_map/all_gather | solution.py:29
  569.4 19.9 %all-gather.5.cloned.1.call-done = bf16[32,64,576]{2,1,0:T(8,128)(2,1)} async-done(((bf16[1,64,576]{2,1,0:T(8,128)(2,1)}), bf16[32,64,576]{2,1,0:T(8,128)(2,1)}) %all-gather.5.cloned.1.call-update) | async-done | bytes 2359312 | tf_op jit(solution)/shard_map/all_gather | solution.py:28
  589.3 2.9 broadcast.110
  592.3 11.5 %while.29 = (s32[]{:T(128)}, f32[32,64,576]{2,1,0:T(8,128)}, f32[8,64,576]{2,1,0:T(8,128)S(1)}, s32[]{:T(128)}, s32[1,1,16]{2,1,0:T(1,128)S(1)}, /*index=5*/s32[...) while((s32[]{:T(128)}, f32[32,64,576]{2,1,0:T(8,128)}, ...), condition=%wide.region_14.18_spmd, body=%wide.region_11.17_spmd.sunk | while | flops 85082160 | bytes 2297161 | solution.py:53
  597.8 2.7 fusion.110
  601.2 2.0 fusion.111
  604.9 4.4 convert_element_type.36
  609.6 193.1 %reduce-scatter.11.cloned.1.call-done = bf16[1,64,576]{2,1,0:T(8,128)(2,1)} async-done(((bf16[8,64,576]{2,1,0:T(8,128)(2,1)}), bf16[1,64,576]{2,1,0:T(8,128)(2,1)}) %reduce-scatter.11.cloned.1.call-update) | async-done | bytes 73744 | tf_op jit(solution)/shard_map/reduce_scatter | solution.py:57
  802.7 89.6 %reduce-scatter.9.cloned.1.call-done = bf16[1,64,576]{2,1,0:T(8,128)(2,1)} async-done(((bf16[32,64,576]{2,1,0:T(8,128)(2,1)}), bf16[1,64,576]{2,1,0:T(8,128)(2,1)}) %reduce-scatter.9.cloned.1.call-update) | async-done | bytes 73744 | tf_op jit(solution)/shard_map/reduce_scatter | solution.py:54
  892.3 1.3 fusion.39
  893.9 74.0 %psum.31 = f32[64,64]{0,1:T(8,128)S(1)} all-reduce(f32[64,64]{0,1:T(8,128)S(1)} %fusion.43), channel_id=1, replica_groups=mesh['row'=8,'col'=32] {'row','col'}, use_global_device_ids=true, to_apply=%region_17.21 | all-reduce | flops 4096 | bytes 32768 | tf_op jit(solution)/shard_map/psum | solution.py:24
  968.0 5.8 cholesky.81
  975.2 4.9 custom-call.17
  980.5 1.0 fusion.34
  981.5 1.0 fusion.32
  (65 shorter events, 14.8 us)
Async XLA Ops:
  7.2 358.8 %copy-start = (bf16[1,576,576]{2,1,0:T(8,128)(2,1)S(1)}, bf16[1,576,576]{2,1,0:T(8,128)(2,1)}, u32[]{:S(2)}) copy-start(bf16[1,576,576]{2,1,0:T(8,128)(2,1)} %param.24) | copy-start | bytes 1990660
  7.2 59.1 %copy-start.6 = (s32[3]{0:T(128)S(1)}, s32[3]{0:T(128)}, u32[]{:S(2)}) copy-start(s32[3]{0:T(128)} %constant.124.clone.1) | copy-start | bytes 40
  7.2 59.1 %copy-start.7 = (s32[3]{0:T(128)S(1)}, s32[3]{0:T(128)}, u32[]{:S(2)}) copy-start(s32[3]{0:T(128)} %constant.127.clone.1) | copy-start | bytes 40
  7.2 59.1 %copy-start.4 = (s32[1,1,16]{2,1,0:T(1,128)S(1)}, s32[1,1,16]{2,1,0:T(1,128)}, u32[]{:S(2)}) copy-start(s32[1,1,16]{2,1,0:T(1,128)} %param.26) | copy-start | bytes 196
  7.2 59.1 %copy-start.5 = (s32[1,1,16]{2,1,0:T(1,128)S(1)}, s32[1,1,16]{2,1,0:T(1,128)}, u32[]{:S(2)}) copy-start(s32[1,1,16]{2,1,0:T(1,128)} %param.27) | copy-start | bytes 196
  7.2 56.0 %all-gather.3.cloned.1.call-start = ((), (), s32[]{:S(2)}) async-start(), calls=%async_computation.4 | async-start | bytes 2703360 | tf_op jit(solution)/shard_map/all_gather | solution.py:28
  8.9 267.8 %reduce-scatter.7.cloned.1.call-start = ((), (), s32[]{:S(2)}) async-start(), calls=%async_computation.6 | async-start | bytes 737280 | tf_op jit(solution)/shard_map/reduce_scatter | solution.py:57
  78.8 287.1 %reduce-scatter.5.cloned.1.call-start = ((), (), s32[]{:S(2)}) async-start(), calls=%async_computation.5 | async-start | bytes 2703360 | tf_op jit(solution)/shard_map/reduce_scatter | solution.py:54
  78.9 4.5 copy-start.1
  78.9 287.1 %copy-start.3 = (bf16[1,64,576]{2,1,0:T(8,128)(2,1)S(1)}, bf16[1,64,576]{2,1,0:T(8,128)(2,1)}, u32[]{:S(2)}) copy-start(bf16[1,64,576]{2,1,0:T(8,128)(2,1)} %convert_element_type.30) | copy-start | bytes 221188
  83.3 505.9 %all-gather.5.cloned.1.call-start = ((), (), s32[]{:S(2)}) async-start(), calls=%async_computation.7 | async-start | bytes 2703360 | tf_op jit(solution)/shard_map/all_gather | solution.py:28
  543.2 259.6 %reduce-scatter.11.cloned.1.call-start = ((), (), s32[]{:S(2)}) async-start(), calls=%async_computation.9 | async-start | bytes 737280 | tf_op jit(solution)/shard_map/reduce_scatter | solution.py:57
  604.8 287.5 %reduce-scatter.9.cloned.1.call-start = ((), (), s32[]{:S(2)}) async-start(), calls=%async_computation.8 | async-start | bytes 2703360 | tf_op jit(solution)/shard_map/reduce_scatter | solution.py:54
  604.8 287.5 %copy-start.2 = (bf16[1,64,576]{2,1,0:T(8,128)(2,1)S(1)}, bf16[1,64,576]{2,1,0:T(8,128)(2,1)}, u32[]{:S(2)}) copy-start(bf16[1,64,576]{2,1,0:T(8,128)(2,1)} %get-tuple-element.197) | copy-start | bytes 221188
Sparse Core Ops, SparseCore 0:
  11.2 52.0 all-gather.2
  79.0 197.7 reduce-scatter.6
  280.6 85.2 reduce-scatter.4
  543.3 45.9 all-gather.4
  604.9 197.7 reduce-scatter.10
  807.0 85.3 reduce-scatter.8
where the time goes:
time: 997 us; the launch traced here: 989 us
  waiting for transfers between devices  610 us (61%)
  blocking collectives  278 us (28%)
  other arithmetic  51.3 us (5%)
  matrix products  18 us (2%)
  between operations  14.4 us (1%)
    reduce_scatter x2, waiting for transfers between devices, apply_operator(): lax.psum_scatter(acc_col.astype(jnp.bfloat16), 'row', scatter_dimension=0...  386 us
    reduce_scatter x2, waiting for transfers between devices, apply_operator(): lax.psum_scatter(acc_row.astype(jnp.bfloat16), 'col', scatter_dimension=0...  179 us
    psum x1, blocking collectives, body(): norm_next = lax.psum(gram_local(residual, residual), ('row', 'col'))  74.6 us
    psum x1, blocking collectives, body(): norm_now = lax.psum(gram_local(residual, residual), ('row', 'col'))  74.1 us
    psum x1, blocking collectives, curvature_sum(): return lax.psum(gram_local(direction, image), ('row', 'col'))  74 us
    all_gather x2, blocking collectives, apply_operator(): col_probe = lax.all_gather(rounded, 'row', axis=0, tiled=True)  55.7 us
    all_gather x2, waiting for transfers between devices, apply_operator(): row_probe = lax.all_gather(rounded, 'col', axis=0, tiled=True)  44.6 us
  transfers between devices with their start and end apart: 6, of which 6 were waited for; matrix products, arithmetic and copies ran while one was open for 1% of the time, Pallas kernels for 0%

commit v1 on v0

v1 whole, which is shorter than its diff:
```python
import jax
import jax.numpy as jnp
from jax import lax
from jax.experimental import pallas as pl
from jax.experimental.pallas import tpu as pltpu
from jax.sharding import PartitionSpec as P

MESH = pl.DeviceIdType.MESH
B, Q, SLOTS, ROWS, PLANE = 576, 64, 16, 8, 32
PK, HALF = 288, 144
STEPS = (1, 3, 2)
N_COPIES = 220
NT = 256


def pack(v):
    tail = jnp.concatenate([v[0:32, 512:576], v[32:64, 512:576]], axis=1)
    return jnp.concatenate(
        [v[:, 0:128], v[:, 128:256], v[:, 256:384], v[:, 384:512], tail], axis=0
    )


def unpack(w):
    tail = jnp.concatenate([w[256:288, 0:64], w[256:288, 64:128]], axis=0)
    return jnp.concatenate(
        [w[0:64], w[64:128], w[128:192], w[192:256], tail], axis=1
    )


def dot(a, b, ca, cb):
    return lax.dot_general(
        a, b, (((ca,), (cb,)), ((), ())), preferred_element_type=jnp.float32
    )


def dot_hi(a, b, ca, cb):
    return lax.dot_general(
        a, b, (((ca,), (cb,)), ((), ())),
        precision=lax.Precision.HIGHEST, preferred_element_type=jnp.float32,
    )


def gram(a, b):
    return dot_hi(a, b, 1, 1)


def combine(coef, block):
    return dot_hi(coef, block, 0, 0)


def solve(matrix, rhs):
    i = lax.broadcasted_iota(jnp.int32, (Q, Q), 0)
    j = lax.broadcasted_iota(jnp.int32, (Q, Q), 1)
    sym = jnp.where(i >= j, matrix, matrix.T)
    work = jnp.concatenate([sym, rhs], axis=1)
    lane = lax.broadcasted_iota(jnp.int32, (Q, 2 * Q), 0)
    for k in range(Q):
        row = work[k : k + 1, :] * (1.0 / work[k : k + 1, k : k + 1])
        work = jnp.where(lane == k, row, work - work[:, k : k + 1] * row)
    return work[:, Q:]


def kernel(
    rows_ref, cols_ref, counts_ref, tiles_ref, diag_ref, probes_ref,
    sol_ref, res_ref,
    blocks, diag, rp_a, rp_b, cp_a, cp_b, ps, xb, qb, r1, sb, r2, pz, zq, zr1, zh, zr2,
    seg_r, seg_c, prev_r, prev_c, last_r, last_c,
    ar0, ar0r, ar1, ar1r, ar2, ar2r,
    send_sem, recv_sem, tile_sem, diag_sem,
):
    z = lax.axis_index("row")
    c = lax.axis_index("col")
    y, x, k = c // 8, (c // 2) % 4, c % 2

    def at(dz=0, dy=0, dx=0, flip=False):
        kk = 1 - k if flip else k
        return (
            lax.rem(z + dz + 8, 8),
            (lax.rem(y + dy + 4, 4) * 4 + lax.rem(x + dx + 4, 4)) * 2 + kk,
        )

    def wrap(v, n):
        return lax.rem(v + 2 * n, n)

    plane_of = {0: lambda d: at(dx=d), 1: lambda d: at(dy=d)}
    used = []
    rps, cps = (rp_a, rp_b), (cp_a, cp_b)

    def send(src, dst, device):
        i = len(used)
        copy = pltpu.make_async_remote_copy(
            src_ref=src, dst_ref=dst, send_sem=send_sem.at[i], recv_sem=recv_sem.at[i],
            device_id=device, device_id_type=MESH,
        )
        used.append(copy)
        copy.start()
        return copy

    tile_copies = [
        pltpu.make_async_copy(tiles_ref.at[0, 0, s], blocks.at[s], tile_sem.at[s])
        for s in range(SLOTS)
    ]
    diag_copy = pltpu.make_async_copy(diag_ref.at[0], diag, diag_sem.at[0])
    diag_copy.start()
    for copy in tile_copies:
        copy.start()

    peers = [at(dx=d) for d in STEPS] + [at(dy=d) for d in STEPS]
    peers += [at(dz=d) for d in range(1, 8)] + [at(flip=True)]
    barrier = pltpu.get_barrier_semaphore()
    for peer in peers:
        pl.semaphore_signal(barrier, inc=1, device_id=peer, device_id_type=MESH)
    pl.semaphore_wait(barrier, len(peers))

    def half(h):
        return pl.ds(h * HALF, HALF)

    def gather_begin(p, value):
        rps[p][k, y, x] = value
        cps[p][z] = value
        first, second, far = [], [], []
        for h in range(2):
            own = rps[p].at[k, y, x, half(h)]
            first.append([send(own, own, plane_of[h](d)) for d in STEPS])
        own = cps[p].at[z]
        for d in (2, -2, 1, -1):
            far.append(send(own, own, at(dz=d)))
        for h in range(2):
            own = rps[p].at[k, y, x, half(h)]
            second.append([[send(own, own, plane_of[1 - h](e)) for e in STEPS]])
        return first, second, far

    def gather_forward(p, state):
        first, second, far = state
        for i, d in enumerate(STEPS):
            for h in range(2):
                first[h][i].wait_recv()
                ty, tx = (y, wrap(x - d, 4)) if h == 0 else (wrap(y - d, 4), x)
                got = rps[p].at[k, ty, tx, half(h)]
                second[h].append([send(got, got, plane_of[1 - h](e)) for e in STEPS])
        for i, d in enumerate((2, -2)):
            far[i].wait_recv()
            got = cps[p].at[wrap(z - d, 8)]
            far.append(send(got, got, at(dz=d // 2)))
            got = cps[p].at[wrap(z - d, 8), half(i)]
            far.append(send(got, got, at(dz=d)))
        third = []
        for h in range(2):
            group = rps[p].at[k, y, :, half(h)] if h == 0 else rps[p].at[k, :, x, half(h)]
            third.append(send(group, group, at(flip=True)))
        return first, second, far, third

    def gather_across(p, state):
        first, second, far, third = state
        for j, e in enumerate(STEPS):
            for h in range(2):
                for part in second[h]:
                    part[j].wait_recv()
                group = (
                    rps[p].at[k, wrap(y - e, 4), :, half(h)]
                    if h == 0
                    else rps[p].at[k, :, wrap(x - e, 4), half(h)]
                )
                third.append(send(group, group, at(flip=True)))

    def gather_end_z(state):
        far = state[2]
        for copy in far[2:]:
            copy.wait_recv()

    def gather_end_plane(state):
        for copy in state[3]:
            copy.wait_recv()

    def forward_products(p):
        @pl.loop(0, SLOTS)
        def _(s):
            far = unpack(cps[p][cols_ref[0, 0, s]])
            seg_r[s] = pack(dot(far, blocks[s], 1, 1)) + seg_r[prev_r[s]]

    def mirror_products(p):
        @pl.loop(0, SLOTS)
        def _(s):
            t = rows_ref[0, 0, s]
            near = unpack(rps[p][lax.rem(t, 2), t // 8, lax.rem(t // 2, 4)])
            seg_c[s] = pack(dot(near, blocks[s], 1, 0)) + seg_c[prev_c[s]]

    def plane_begin(p):
        def fill(kk):
            @pl.loop(0, 16)
            def _(t):
                ps[p, kk, t // 4, lax.rem(t, 4)] = seg_r[last_r[2 * t + kk]].astype(jnp.bfloat16)

        fill(1 - k)
        out = []
        for e in (2, 1, 3, 0):
            for h in range(2):
                if h == 0:
                    t = wrap(y + e, 4)
                    src, dst = ps.at[p, 1 - k, t, :, half(h)], xb.at[p, t, :, half(h)]
                else:
                    t = wrap(x + e, 4)
                    src, dst = ps.at[p, 1 - k, :, t, half(h)], xb.at[p, :, t, half(h)]
                out.append(send(src, dst, at(flip=True)))
        fill(k)
        return out

    def plane_stage(p, across):
        out = [[], []]
        n = 0
        for e in (2, 1, 3, 0):
            for h in range(2):
                across[n].wait_recv()
                n += 1
                if h == 0:
                    t = wrap(y + e, 4)
                    total = ps[p, k, t, :, half(h)].astype(jnp.float32) + xb[p, t, :, half(h)].astype(jnp.float32)
                else:
                    t = wrap(x + e, 4)
                    total = ps[p, k, :, t, half(h)].astype(jnp.float32) + xb[p, :, t, half(h)].astype(jnp.float32)
                qb[p, h, e] = total.astype(jnp.bfloat16)
                if e != 0:
                    out[h].append(send(qb.at[p, h, e], r1.at[p, h, e - 1], plane_of[1 - h](e)))
        return out

    def plane_stage2(p, mid):
        out = [[], []]
        for h in range(2):
            for copy in mid[h]:
                copy.wait_recv()
            total = qb[p, h, 0].astype(jnp.float32)
            for e in range(3):
                total = total + r1[p, h, e].astype(jnp.float32)
            sb[p, h] = total.astype(jnp.bfloat16)
            at_axis = x if h == 0 else y
            for d in (1, 2, 3):
                out[h].append(send(sb.at[p, h, wrap(at_axis + d, 4)], r2.at[p, h, d - 1], plane_of[h](d)))
        return out

    def plane_end(p, last):
        halves = []
        for h in range(2):
            total = sb[p, h, x if h == 0 else y].astype(jnp.float32)
            for d in range(3):
                last[h][d].wait_recv()
                total = total + r2[p, h, d].astype(jnp.float32)
            halves.append(total)
        return jnp.concatenate(halves, axis=0)

    def z_begin(p):
        @pl.loop(0, ROWS)
        def _(t):
            pz[p, t] = seg_c[last_c[t]].astype(jnp.bfloat16)

        out = [
            send(pz.at[p, wrap(z + 3, 8)], zr1.at[p, 0], at(dz=1)),
            send(pz.at[p, wrap(z - 3, 8)], zr1.at[p, 1], at(dz=-1)),
            send(pz.at[p, wrap(z + 4, 8), half(0)], zh.at[p, 0], at(dz=2)),
            send(pz.at[p, wrap(z + 4, 8), half(1)], zh.at[p, 1], at(dz=-2)),
            send(pz.at[p, wrap(z + 1, 8)], zr2.at[p, 0], at(dz=1)),
            send(pz.at[p, wrap(z - 1, 8)], zr2.at[p, 1], at(dz=-1)),
        ]
        return out

    def z_stage(p, out):
        for i, d in enumerate((2, -2)):
            out[i].wait_recv()
            out[2 + i].wait_recv()
            total = pz[p, wrap(z + d, 8)].astype(jnp.float32) + zr1[p, i].astype(jnp.float32)
            extra = zh[p, i].astype(jnp.float32)
            lo, hi = total[0:HALF], total[HALF:PK]
            if i == 0:
                lo = lo + extra
            else:
                hi = hi + extra
            zq[p, i, 0:HALF] = lo.astype(jnp.bfloat16)
            zq[p, i, HALF:PK] = hi.astype(jnp.bfloat16)
            out.append(send(zq.at[p, i], zr2.at[p, 2 + i], at(dz=d)))

    def z_end(p, out):
        total = pz[p, z].astype(jnp.float32)
        for i in range(4):
            out[4 + i].wait_recv()
            total = total + zr2[p, i].astype(jnp.float32)
        return total

    groups = (
        [at(flip=True)],
        [at(dx=d) for d in STEPS],
        [at(dy=d) for d in STEPS],
        [at(dz=d) for d in range(1, 8)],
    )
    bases = (0, 1, 4, 7)

    def reduce_start(buf, rbuf, stage):
        return [
            send(buf.at[stage], rbuf.at[bases[stage] + i], peer)
            for i, peer in enumerate(groups[stage])
        ]

    def reduce_finish(buf, rbuf, stage, copies):
        total = buf[stage]
        for i, copy in enumerate(copies):
            copy.wait_recv()
            total = total + rbuf[bases[stage] + i]
        if stage < 3:
            buf[stage + 1] = total
        return total

    def own_product(v):
        hi = v.astype(jnp.bfloat16)
        lo = (v - hi.astype(jnp.float32)).astype(jnp.bfloat16)
        d = diag[...]
        return dot(hi, d, 1, 1) + dot(lo, d, 1, 1)

    probes = probes_ref[0]
    state = gather_begin(0, pack(probes).astype(jnp.bfloat16))

    count = counts_ref[0, 0]
    for s in range(SLOTS):
        pr = jnp.int32(SLOTS)
        pc = jnp.int32(SLOTS)
        for u in range(s):
            pr = jnp.where(rows_ref[0, 0, u] == rows_ref[0, 0, s], u, pr)
            pc = jnp.where(cols_ref[0, 0, u] == cols_ref[0, 0, s], u, pc)
        prev_r[s] = pr
        prev_c[s] = pc

    @pl.loop(0, PLANE)
    def _(t):
        at_slot = jnp.int32(SLOTS)
        for s in range(SLOTS):
            at_slot = jnp.where((rows_ref[0, 0, s] == t) & (s < count), s, at_slot)
        last_r[t] = at_slot

    @pl.loop(0, ROWS)
    def _(t):
        at_slot = jnp.int32(SLOTS)
        for s in range(SLOTS):
            at_slot = jnp.where((cols_ref[0, 0, s] == t) & (s < count), s, at_slot)
        last_c[t] = at_slot

    seg_r[SLOTS] = jnp.zeros((PK, 128), jnp.float32)
    seg_c[SLOTS] = jnp.zeros((PK, 128), jnp.float32)

    diag_copy.wait()
    own = own_product(probes)
    trace = jnp.float32(0.0)
    for j in range(5):
        n = 128 if j < 4 else 64
        d = diag[pl.ds(128 * j, n), pl.ds(128 * j, n)].astype(jnp.float32)
        eye = lax.broadcasted_iota(jnp.int32, (n, n), 0) == lax.broadcasted_iota(jnp.int32, (n, n), 1)
        trace = trace + jnp.sum(jnp.where(eye, d, 0.0), keepdims=True)
    g00 = gram(probes, probes)
    ar0[0, 0:64] = jnp.concatenate([g00, jnp.broadcast_to(trace, (Q, Q))], axis=1)
    red = reduce_start(ar0, ar0r, 0)
    state = gather_forward(0, state)
    reduce_finish(ar0, ar0r, 0, red)
    red = reduce_start(ar0, ar0r, 1)
    gather_across(0, state)
    gather_end_z(state)
    reduce_finish(ar0, ar0r, 1, red)
    red = reduce_start(ar0, ar0r, 2)
    for copy in tile_copies:
        copy.wait()
    forward_products(0)
    across = plane_begin(0)
    gather_end_plane(state)
    mirror_products(0)
    zs = z_begin(0)
    reduce_finish(ar0, ar0r, 2, red)
    red = reduce_start(ar0, ar0r, 3)
    mid = plane_stage(0, across)
    z_stage(0, zs)
    last = plane_stage2(0, mid)
    total = reduce_finish(ar0, ar0r, 3, red)
    rr0 = total[:, 0:Q]
    shift = total[0:1, Q : Q + 1] * (1.0 / (NT * B))
    image = z_end(0, zs)
    image = image + plane_end(0, last)
    image = own + unpack(image)
    basis = image - shift * probes

    state = gather_begin(1, pack(basis).astype(jnp.bfloat16))
    g01 = gram(probes, basis)
    g11 = gram(basis, basis)
    ar1[0, 0:64] = jnp.concatenate([g01, g11], axis=1)
    red = reduce_start(ar1, ar1r, 0)
    own = own_product(basis)
    state = gather_forward(1, state)
    reduce_finish(ar1, ar1r, 0, red)
    red = reduce_start(ar1, ar1r, 1)
    gather_across(1, state)
    gather_end_z(state)
    reduce_finish(ar1, ar1r, 1, red)
    red = reduce_start(ar1, ar1r, 2)
    forward_products(1)
    across = plane_begin(1)
    gather_end_plane(state)
    mirror_products(1)
    zs = z_begin(1)
    reduce_finish(ar1, ar1r, 2, red)
    red = reduce_start(ar1, ar1r, 3)
    mid = plane_stage(1, across)
    z_stage(1, zs)
    total = reduce_finish(ar1, ar1r, 3, red)
    g01, g11 = total[:, 0:Q], total[:, Q:]
    eye = (
        lax.broadcasted_iota(jnp.int32, (Q, Q), 0) == lax.broadcasted_iota(jnp.int32, (Q, Q), 1)
    ).astype(jnp.float32)
    alpha = solve(g01 + shift * rr0, rr0)
    m0 = eye - shift * alpha
    m1 = -alpha
    rr1 = (
        dot_hi(m0, dot_hi(rr0, m0, 1, 0) + dot_hi(g01, m1, 1, 0), 0, 0)
        + dot_hi(m1, dot_hi(g01, m0, 0, 0) + dot_hi(g11, m1, 1, 0), 0, 0)
    )
    beta = solve(rr0, rr1)
    n0 = m0 + beta
    last = plane_stage2(1, mid)
    residual = combine(m0, probes) + combine(m1, basis)
    direction = residual + combine(beta, probes)
    xsol = combine(alpha, probes)
    partial = combine(n0, image)
    deep = z_end(1, zs)
    deep = deep + plane_end(1, last)
    deep = own + unpack(deep)
    image2 = partial + combine(m1, deep)
    pq = gram(direction, image2)
    ar2[0, 0:32] = jnp.concatenate([pq[0:32], pq[32:64]], axis=1)
    for stage in range(4):
        red = reduce_start(ar2, ar2r, stage)
        total = reduce_finish(ar2, ar2r, stage, red)
    pq = jnp.concatenate([total[:, 0:Q], total[:, Q:]], axis=0)
    gamma = solve(pq, rr1)
    sol_ref[0] = xsol + combine(gamma, direction)
    res_ref[0] = residual - combine(gamma, image2)
    for copy in used:
        copy.wait_send()


def body(tiles, diag_tiles, probes, rows_list, cols_list, counts):
    smem = pl.BlockSpec(memory_space=pltpu.SMEM)
    vmem = pl.BlockSpec(memory_space=pltpu.VMEM)
    hbm = pl.BlockSpec(memory_space=pl.ANY)
    bf, f32, i32 = jnp.bfloat16, jnp.float32, jnp.int32
    return pl.pallas_call(
        kernel,
        out_shape=(jax.ShapeDtypeStruct((1, Q, B), f32),) * 2,
        in_specs=[smem, smem, smem, hbm, hbm, vmem],
        out_specs=(vmem, vmem),
        scratch_shapes=[
            pltpu.VMEM((SLOTS, B, B), bf),
            pltpu.VMEM((B, B), bf),
            pltpu.VMEM((2, 4, 4, PK, 128), bf),
            pltpu.VMEM((2, 4, 4, PK, 128), bf),
            pltpu.VMEM((ROWS, PK, 128), bf),
            pltpu.VMEM((ROWS, PK, 128), bf),
            pltpu.VMEM((2, 2, 4, 4, PK, 128), bf),
            pltpu.VMEM((2, 4, 4, PK, 128), bf),
            pltpu.VMEM((2, 2, 4, 4, HALF, 128), bf),
            pltpu.VMEM((2, 2, 3, 4, HALF, 128), bf),
            pltpu.VMEM((2, 2, 4, HALF, 128), bf),
            pltpu.VMEM((2, 2, 3, HALF, 128), bf),
            pltpu.VMEM((2, ROWS, PK, 128), bf),
            pltpu.VMEM((2, 2, PK, 128), bf),
            pltpu.VMEM((2, 2, PK, 128), bf),
            pltpu.VMEM((2, 2, HALF, 128), bf),
            pltpu.VMEM((2, 4, PK, 128), bf),
            pltpu.VMEM((SLOTS + 1, PK, 128), f32),
            pltpu.VMEM((SLOTS + 1, PK, 128), f32),
            pltpu.SMEM((SLOTS,), i32),
            pltpu.SMEM((SLOTS,), i32),
            pltpu.SMEM((PLANE,), i32),
            pltpu.SMEM((ROWS,), i32),
            pltpu.VMEM((4, 64, 128), f32),
            pltpu.VMEM((14, 64, 128), f32),
            pltpu.VMEM((4, 64, 128), f32),
            pltpu.VMEM((14, 64, 128), f32),
            pltpu.VMEM((4, 32, 128), f32),
            pltpu.VMEM((14, 32, 128), f32),
            pltpu.SemaphoreType.DMA((N_COPIES,)),
            pltpu.SemaphoreType.DMA((N_COPIES,)),
            pltpu.SemaphoreType.DMA((SLOTS,)),
            pltpu.SemaphoreType.DMA((1,)),
        ],
        compiler_params=pltpu.CompilerParams(
            collective_id=0, has_side_effects=True, vmem_limit_bytes=56 << 20
        ),
        name="block_cg",
    )(rows_list, cols_list, counts, tiles, diag_tiles, probes)


def solution(mesh):
    placed = (
        P("row", "col", None, None, None),
        P(("row", "col"), None, None),
        P(("row", "col"), None, None),
        P("row", "col", None),
        P("row", "col", None),
        P("row", "col"),
    )
    return jax.shard_map(
        body,
        mesh=mesh,
        in_specs=placed,
        out_specs=(P(("row", "col"), None, None), P(("row", "col"), None, None)),
        check_vma=False,
    )
```

time: 997 us -> 134 us (0.13)
  waiting for transfers between devices: 610 us -> 0 us
  blocking collectives: 278 us -> 0 us
  Pallas kernels: 0 us -> 128 us
  other arithmetic: 51.3 us -> 0 us
  matrix products: 18 us -> 0 us
  between operations: 14.4 us -> 1.29 us
    reduce_scatter x4 -> x0, waiting for transfers between devices: 565 us -> none  [the longest x2 386 us: apply_operator(): lax.psum_scatter(acc_col.astype(jnp.bfloat16), 'row', scatter_dimension=0...]
    psum x3 -> x0, blocking collectives: 223 us -> none  [the longest x1 74.6 us: body(): norm_next = lax.psum(gram_local(residual, residual), ('row', 'col'))]
    pallas_call x0 -> x1, Pallas kernels: none -> 128 us  [body(): pl.pallas_call(kernel, out_shape=(jax.ShapeDtypeStruct((1, Q, B), f32),)...]
    all_gather x2 -> x0, blocking collectives: 55.7 us -> none  [apply_operator(): col_probe = lax.all_gather(rounded, 'row', axis=0, tiled=True)]
    all_gather x2 -> x0, waiting for transfers between devices: 44.6 us -> none  [apply_operator(): row_probe = lax.all_gather(rounded, 'col', axis=0, tiled=True)]
    another operation x19 -> x0, other arithmetic: 38.9 us -> none  [the longest x9 19.6 us: solve_with(): factor = jnp.linalg.cholesky(matrix)]
    dot_general x15 -> x0, matrix products: 16.8 us -> none  [the longest x2 5.39 us: turn(): lax.dot_general(far, block, (((1,), (1,)), ((), ())), preferred_element_t...]
    convert_element_type x5 -> x0, other arithmetic: 12.3 us -> none  [the longest x2 8.8 us: apply_operator(): acc_row.astype(jnp.bfloat16)]
  transfers between devices with their start and end apart: 6 -> 0, of which waited for: 6 -> 0; matrix products, arithmetic and copies ran while one was open for 1% -> 0% of each run, Pallas kernels for 0% -> 0%
where the time goes in v1:
time: 134 us; the launch traced here: 133 us
  Pallas kernels  128 us (96%)
  local copies, waits for them, and re-layouts  3.18 us (2%)
    pallas_call x1, Pallas kernels, body(): pl.pallas_call(kernel, out_shape=(jax.ShapeDtypeStruct((1, Q, B), f32),)...  128 us
    unnamed x2, local copies, waits for them, and re-layouts  3.18 us

profile of v1, /device:TPU:8, one launch (start us, length us, event | category | flops | bytes accessed | tf_op | source)
XLA Modules:
  0.0 132.7 jit_solution(3912590105819589344)
XLA Ops:
  1.3 128.2 %block_cg.1 = (f32[1,64,576]{2,1,0:T(8,128)}, f32[1,64,576]{2,1,0:T(8,128)}) custom-call(s32[1,1,16]{2,1,0:T(1,128)} %rows_ref.1, s32[1,1,16]{2,1,0:T(1,128)} %cols_ref.1, s32[1,1]{1,0:T(1,128)S(6)} %copy.10.counts_ref, bf16[1,1,16,576,576]{4,3,2,1,0:T(8,128)(2,1)} %tiles_ref.1, bf16[1,576,576]{2,1,0:T(8,128)(2,1)} %diag_ref.1, f32[1,64,576]{2,1,0:T(8,128)} %probes_ref.1), custom_call_target="tpu_custom_call" | custom-call | tf_op jit(solution)/shard_map/block_cg/pallas_call | solution.py:447
  129.5 1.6 %copy.11 = f32[1,64,576]{2,1,0:T(8,128)} copy(f32[1,64,576]{2,1,0:T(8,128)} %get-tuple-element.4) | data formatting | bytes 294912
  131.1 1.6 %copy.12 = f32[1,64,576]{2,1,0:T(8,128)} copy(f32[1,64,576]{2,1,0:T(8,128)} %get-tuple-element.5) | data formatting | bytes 294912

commit v2 on v1

--- a/solution.py
+++ b/solution.py
@@ -9,8 +9,9 @@
 B, Q, SLOTS, ROWS, PLANE = 576, 64, 16, 8, 32
 PK, HALF = 288, 144
 STEPS = (1, 3, 2)
-N_COPIES = 220
+N_COPIES = 248
 NT = 256
+UNROLL = 4
 
 
 def pack(v):
@@ -53,11 +54,38 @@
     j = lax.broadcasted_iota(jnp.int32, (Q, Q), 1)
     sym = jnp.where(i >= j, matrix, matrix.T)
     work = jnp.concatenate([sym, rhs], axis=1)
-    lane = lax.broadcasted_iota(jnp.int32, (Q, 2 * Q), 0)
-    for k in range(Q):
-        row = work[k : k + 1, :] * (1.0 / work[k : k + 1, k : k + 1])
-        work = jnp.where(lane == k, row, work - work[:, k : k + 1] * row)
+    line = lax.broadcasted_iota(jnp.int32, (Q, 2 * Q), 0)
+    n = 8
+    for k in range(0, Q, n):
+        col = [jnp.broadcast_to(work[:, k + a : k + a + 1], (Q, 2 * Q)) for a in range(n)]
+        row = [work[k + a : k + a + 1, :] for a in range(n)]
+        piv = [[col[b][k + a : k + a + 1, :] for b in range(n)] for a in range(n)]
+        for a in range(n):
+            inv = 1.0 / piv[a][a]
+            row[a] = row[a] * inv
+            for b in range(a + 1, n):
+                piv[a][b] = piv[a][b] * inv
+            for other in range(n):
+                if other != a:
+                    f = piv[other][a]
+                    row[other] = row[other] - f * row[a]
+                    for b in range(a + 1, n):
+                        piv[other][b] = piv[other][b] - f * piv[a][b]
+        new = work
+        for a in range(n):
+            new = new - col[a] * row[a]
+        for a in range(n):
+            new = jnp.where(line == k + a, row[a], new)
+        work = new
     return work[:, Q:]
+
+
+def fold(g):
+    return jnp.concatenate([g[0:32], g[32:64]], axis=1)
+
+
+def unfold(g):
+    return jnp.concatenate([g[:, 0:Q], g[:, Q:]], axis=0)
 
 
 def kernel(
@@ -65,7 +93,7 @@
     sol_ref, res_ref,
     blocks, diag, rp_a, rp_b, cp_a, cp_b, ps, xb, qb, r1, sb, r2, pz, zq, zr1, zh, zr2,
     seg_r, seg_c, prev_r, prev_c, last_r, last_c,
-    ar0, ar0r, ar1, ar1r, ar2, ar2r,
+    ar_a, ar_ar, ar_b, ar_br, ar_c, ar_cr, ar_d, ar_dr,
     send_sem, recv_sem, tile_sem, diag_sem,
 ):
     z = lax.axis_index("row")
@@ -101,9 +129,6 @@
         for s in range(SLOTS)
     ]
     diag_copy = pltpu.make_async_copy(diag_ref.at[0], diag, diag_sem.at[0])
-    diag_copy.start()
-    for copy in tile_copies:
-        copy.start()
 
     peers = [at(dx=d) for d in STEPS] + [at(dy=d) for d in STEPS]
     peers += [at(dz=d) for d in range(1, 8)] + [at(flip=True)]
@@ -173,17 +198,27 @@
             copy.wait_recv()
 
     def forward_products(p):
-        @pl.loop(0, SLOTS)
-        def _(s):
+        def step(s, carry):
             far = unpack(cps[p][cols_ref[0, 0, s]])
             seg_r[s] = pack(dot(far, blocks[s], 1, 1)) + seg_r[prev_r[s]]
+            return carry
+
+        lax.fori_loop(0, SLOTS, step, 0, unroll=UNROLL)
 
     def mirror_products(p):
-        @pl.loop(0, SLOTS)
-        def _(s):
+        count = counts_ref[0, 0]
+
+        def step(s, cross):
             t = rows_ref[0, 0, s]
             near = unpack(rps[p][lax.rem(t, 2), t // 8, lax.rem(t // 2, 4)])
-            seg_c[s] = pack(dot(near, blocks[s], 1, 0)) + seg_c[prev_c[s]]
+            far = unpack(cps[p][cols_ref[0, 0, s]])
+            product = dot(near, blocks[s], 1, 0)
+            seg_c[s] = pack(product) + seg_c[prev_c[s]]
+            held = jnp.where(s < count, 1.0, 0.0)
+            return cross + held * dot(far, product.astype(jnp.bfloat16), 1, 1)
+
+        cross = lax.fori_loop(0, SLOTS, step, jnp.zeros((Q, Q), jnp.float32), unroll=UNROLL)
+        return cross + cross.T
 
     def plane_begin(p):
         def fill(kk):
@@ -193,57 +228,61 @@
 
         fill(1 - k)
         out = []
-        for e in (2, 1, 3, 0):
+        for d in (2, 1, 3, 0):
             for h in range(2):
                 if h == 0:
-                    t = wrap(y + e, 4)
+                    t = wrap(x + d, 4)
+                    src, dst = ps.at[p, 1 - k, :, t, half(h)], xb.at[p, :, t, half(h)]
+                else:
+                    t = wrap(y + d, 4)
                     src, dst = ps.at[p, 1 - k, t, :, half(h)], xb.at[p, t, :, half(h)]
-                else:
-                    t = wrap(x + e, 4)
-                    src, dst = ps.at[p, 1 - k, :, t, half(h)], xb.at[p, :, t, half(h)]
                 out.append(send(src, dst, at(flip=True)))
         fill(k)
         return out
 
     def plane_stage(p, across):
-        out = [[], []]
+        out = [{}, {}]
         n = 0
-        for e in (2, 1, 3, 0):
+        for d in (2, 1, 3, 0):
             for h in range(2):
                 across[n].wait_recv()
                 n += 1
                 if h == 0:
-                    t = wrap(y + e, 4)
+                    t, mine = wrap(x + d, 4), y
+                    total = ps[p, k, :, t, half(h)].astype(jnp.float32) + xb[p, :, t, half(h)].astype(jnp.float32)
+                else:
+                    t, mine = wrap(y + d, 4), x
                     total = ps[p, k, t, :, half(h)].astype(jnp.float32) + xb[p, t, :, half(h)].astype(jnp.float32)
-                else:
-                    t = wrap(x + e, 4)
-                    total = ps[p, k, :, t, half(h)].astype(jnp.float32) + xb[p, :, t, half(h)].astype(jnp.float32)
-                qb[p, h, e] = total.astype(jnp.bfloat16)
-                if e != 0:
-                    out[h].append(send(qb.at[p, h, e], r1.at[p, h, e - 1], plane_of[1 - h](e)))
+                qb[p, h, d] = total.astype(jnp.bfloat16)
+                out[h][d] = [
+                    send(qb.at[p, h, d, wrap(mine + e, 4)], r1.at[p, h, d, e - 1], plane_of[1 - h](e))
+                    for e in (2, 1, 3)
+                ]
         return out
 
     def plane_stage2(p, mid):
         out = [[], []]
-        for h in range(2):
-            for copy in mid[h]:
-                copy.wait_recv()
-            total = qb[p, h, 0].astype(jnp.float32)
-            for e in range(3):
-                total = total + r1[p, h, e].astype(jnp.float32)
-            sb[p, h] = total.astype(jnp.bfloat16)
-            at_axis = x if h == 0 else y
-            for d in (1, 2, 3):
-                out[h].append(send(sb.at[p, h, wrap(at_axis + d, 4)], r2.at[p, h, d - 1], plane_of[h](d)))
+        for d in (2, 1, 3, 0):
+            for h in range(2):
+                for copy in mid[h][d]:
+                    copy.wait_recv()
+                total = qb[p, h, d, y if h == 0 else x].astype(jnp.float32)
+                for e in range(3):
+                    total = total + r1[p, h, d, e].astype(jnp.float32)
+                if d != 0:
+                    sb[p, h, d] = total.astype(jnp.bfloat16)
+                    out[h].append(send(sb.at[p, h, d], r2.at[p, h, d - 1], plane_of[h](d)))
+                else:
+                    out[h].append(total)
         return out
 
     def plane_end(p, last):
         halves = []
         for h in range(2):
-            total = sb[p, h, x if h == 0 else y].astype(jnp.float32)
-            for d in range(3):
-                last[h][d].wait_recv()
-                total = total + r2[p, h, d].astype(jnp.float32)
+            total = last[h][3]
+            for i, d in enumerate((2, 1, 3)):
+                last[h][i].wait_recv()
+                total = total + r2[p, h, d - 1].astype(jnp.float32)
             halves.append(total)
         return jnp.concatenate(halves, axis=0)
 
@@ -292,20 +331,28 @@
     )
     bases = (0, 1, 4, 7)
 
-    def reduce_start(buf, rbuf, stage):
-        return [
-            send(buf.at[stage], rbuf.at[bases[stage] + i], peer)
-            for i, peer in enumerate(groups[stage])
-        ]
-
-    def reduce_finish(buf, rbuf, stage, copies):
-        total = buf[stage]
-        for i, copy in enumerate(copies):
-            copy.wait_recv()
-            total = total + rbuf[bases[stage] + i]
-        if stage < 3:
-            buf[stage + 1] = total
-        return total
+    def reduce_steps(buf, rbuf, value):
+        buf[0, 0 : value.shape[0]] = value
+        for stage in range(4):
+            copies = [
+                send(buf.at[stage], rbuf.at[bases[stage] + i], peer)
+                for i, peer in enumerate(groups[stage])
+            ]
+            yield None
+            total = buf[stage]
+            for i, copy in enumerate(copies):
+                copy.wait_recv()
+                total = total + rbuf[bases[stage] + i]
+            if stage < 3:
+                buf[stage + 1] = total
+        yield total
+
+    drained = [0]
+
+    def drain():
+        for copy in used[drained[0] :]:
+            copy.wait_send()
+        drained[0] = len(used)
 
     def own_product(v):
         hi = v.astype(jnp.bfloat16)
@@ -315,6 +362,9 @@
 
     probes = probes_ref[0]
     state = gather_begin(0, pack(probes).astype(jnp.bfloat16))
+    diag_copy.start()
+    for copy in tile_copies[:8]:
+        copy.start()
 
     count = counts_ref[0, 0]
     for s in range(SLOTS):
@@ -343,100 +393,109 @@
     seg_r[SLOTS] = jnp.zeros((PK, 128), jnp.float32)
     seg_c[SLOTS] = jnp.zeros((PK, 128), jnp.float32)
 
+    g00 = gram(probes, probes)
     diag_copy.wait()
-    own = own_product(probes)
-    trace = jnp.float32(0.0)
+    trace = jnp.zeros((1, 1), jnp.float32)
     for j in range(5):
         n = 128 if j < 4 else 64
         d = diag[pl.ds(128 * j, n), pl.ds(128 * j, n)].astype(jnp.float32)
-        eye = lax.broadcasted_iota(jnp.int32, (n, n), 0) == lax.broadcasted_iota(jnp.int32, (n, n), 1)
-        trace = trace + jnp.sum(jnp.where(eye, d, 0.0), keepdims=True)
-    g00 = gram(probes, probes)
-    ar0[0, 0:64] = jnp.concatenate([g00, jnp.broadcast_to(trace, (Q, Q))], axis=1)
-    red = reduce_start(ar0, ar0r, 0)
+        on = lax.broadcasted_iota(jnp.int32, (n, n), 0) == lax.broadcasted_iota(jnp.int32, (n, n), 1)
+        trace = trace + jnp.sum(jnp.where(on, d, 0.0), keepdims=True)
+    red_a = reduce_steps(
+        ar_a, ar_ar, jnp.concatenate([fold(g00), jnp.broadcast_to(trace, (8, 128))], axis=0)
+    )
+    next(red_a)
     state = gather_forward(0, state)
-    reduce_finish(ar0, ar0r, 0, red)
-    red = reduce_start(ar0, ar0r, 1)
+    for copy in tile_copies[8:]:
+        copy.start()
+    next(red_a)
+    own = own_product(probes)
     gather_across(0, state)
+    next(red_a)
     gather_end_z(state)
-    reduce_finish(ar0, ar0r, 1, red)
-    red = reduce_start(ar0, ar0r, 2)
     for copy in tile_copies:
         copy.wait()
     forward_products(0)
     across = plane_begin(0)
+    next(red_a)
     gather_end_plane(state)
-    mirror_products(0)
+    cross = mirror_products(0)
     zs = z_begin(0)
-    reduce_finish(ar0, ar0r, 2, red)
-    red = reduce_start(ar0, ar0r, 3)
+    red_b = reduce_steps(ar_b, ar_br, fold(gram(probes, own) + cross))
+    next(red_b)
     mid = plane_stage(0, across)
+    total = next(red_a)
+    rr0 = unfold(total[0:32])
+    shift = total[32:33, 0:1] * (1.0 / (NT * B))
     z_stage(0, zs)
+    next(red_b)
+    eye = (
+        lax.broadcasted_iota(jnp.int32, (Q, Q), 0) == lax.broadcasted_iota(jnp.int32, (Q, Q), 1)
+    ).astype(jnp.float32)
+    rr0_inv = solve(rr0, eye)
     last = plane_stage2(0, mid)
-    total = reduce_finish(ar0, ar0r, 3, red)
-    rr0 = total[:, 0:Q]
-    shift = total[0:1, Q : Q + 1] * (1.0 / (NT * B))
+    next(red_b)
     image = z_end(0, zs)
     image = image + plane_end(0, last)
     image = own + unpack(image)
     basis = image - shift * probes
 
     state = gather_begin(1, pack(basis).astype(jnp.bfloat16))
-    g01 = gram(probes, basis)
-    g11 = gram(basis, basis)
-    ar1[0, 0:64] = jnp.concatenate([g01, g11], axis=1)
-    red = reduce_start(ar1, ar1r, 0)
+    next(red_b)
+    red_c = reduce_steps(ar_c, ar_cr, fold(gram(basis, basis)))
+    next(red_c)
     own = own_product(basis)
     state = gather_forward(1, state)
-    reduce_finish(ar1, ar1r, 0, red)
-    red = reduce_start(ar1, ar1r, 1)
+    next(red_c)
+    pq0 = unfold(next(red_b))
+    alpha = solve(pq0, rr0)
+    drain()
     gather_across(1, state)
+    next(red_c)
     gather_end_z(state)
-    reduce_finish(ar1, ar1r, 1, red)
-    red = reduce_start(ar1, ar1r, 2)
     forward_products(1)
     across = plane_begin(1)
+    next(red_c)
     gather_end_plane(state)
-    mirror_products(1)
+    cross = mirror_products(1)
     zs = z_begin(1)
-    reduce_finish(ar1, ar1r, 2, red)
-    red = reduce_start(ar1, ar1r, 3)
+    red_d = reduce_steps(ar_d, ar_dr, fold(gram(basis, own) + cross))
+    next(red_d)
     mid = plane_stage(1, across)
-    z_stage(1, zs)
-    total = reduce_finish(ar1, ar1r, 3, red)
-    g01, g11 = total[:, 0:Q], total[:, Q:]
-    eye = (
-        lax.broadcasted_iota(jnp.int32, (Q, Q), 0) == lax.broadcasted_iota(jnp.int32, (Q, Q), 1)
-    ).astype(jnp.float32)
-    alpha = solve(g01 + shift * rr0, rr0)
+    g11 = unfold(next(red_c))
+    g01 = pq0 - shift * rr0
     m0 = eye - shift * alpha
     m1 = -alpha
     rr1 = (
         dot_hi(m0, dot_hi(rr0, m0, 1, 0) + dot_hi(g01, m1, 1, 0), 0, 0)
         + dot_hi(m1, dot_hi(g01, m0, 0, 0) + dot_hi(g11, m1, 1, 0), 0, 0)
     )
-    beta = solve(rr0, rr1)
+    beta = dot_hi(rr0_inv, rr1, 1, 0)
     n0 = m0 + beta
-    last = plane_stage2(1, mid)
+    z_stage(1, zs)
+    next(red_d)
     residual = combine(m0, probes) + combine(m1, basis)
     direction = residual + combine(beta, probes)
     xsol = combine(alpha, probes)
     partial = combine(n0, image)
+    next(red_d)
+    last = plane_stage2(1, mid)
+    next(red_d)
+    g12 = unfold(next(red_d))
+    g02 = g11 + shift * g01
+    pq1 = (
+        dot_hi(n0, dot_hi(pq0, n0, 1, 0) + dot_hi(g02, m1, 1, 0), 0, 0)
+        + dot_hi(m1, dot_hi(g02, n0, 0, 0) + dot_hi(g12, m1, 1, 0), 0, 0)
+    )
+    gamma = solve(pq1, rr1)
+    sol_ref[0] = xsol + combine(gamma, direction)
+    start = residual - combine(gamma, partial)
+    m2 = dot_hi(m1, gamma, 1, 0)
     deep = z_end(1, zs)
     deep = deep + plane_end(1, last)
     deep = own + unpack(deep)
-    image2 = partial + combine(m1, deep)
-    pq = gram(direction, image2)
-    ar2[0, 0:32] = jnp.concatenate([pq[0:32], pq[32:64]], axis=1)
-    for stage in range(4):
-        red = reduce_start(ar2, ar2r, stage)
-        total = reduce_finish(ar2, ar2r, stage, red)
-    pq = jnp.concatenate([total[:, 0:Q], total[:, Q:]], axis=0)
-    gamma = solve(pq, rr1)
-    sol_ref[0] = xsol + combine(gamma, direction)
-    res_ref[0] = residual - combine(gamma, image2)
-    for copy in used:
-        copy.wait_send()
+    res_ref[0] = start - combine(m2, deep)
+    drain()
 
 
 def body(tiles, diag_tiles, probes, rows_list, cols_list, counts):
@@ -459,7 +518,7 @@
             pltpu.VMEM((2, 2, 4, 4, PK, 128), bf),
             pltpu.VMEM((2, 4, 4, PK, 128), bf),
             pltpu.VMEM((2, 2, 4, 4, HALF, 128), bf),
-            pltpu.VMEM((2, 2, 3, 4, HALF, 128), bf),
+            pltpu.VMEM((2, 2, 4, 3, HALF, 128), bf),
             pltpu.VMEM((2, 2, 4, HALF, 128), bf),
             pltpu.VMEM((2, 2, 3, HALF, 128), bf),
             pltpu.VMEM((2, ROWS, PK, 128), bf),
@@ -473,10 +532,12 @@
             pltpu.SMEM((SLOTS,), i32),
             pltpu.SMEM((PLANE,), i32),
             pltpu.SMEM((ROWS,), i32),
-            pltpu.VMEM((4, 64, 128), f32),
-            pltpu.VMEM((14, 64, 128), f32),
-            pltpu.VMEM((4, 64, 128), f32),
-            pltpu.VMEM((14, 64, 128), f32),
+            pltpu.VMEM((4, 40, 128), f32),
+            pltpu.VMEM((14, 40, 128), f32),
+            pltpu.VMEM((4, 32, 128), f32),
+            pltpu.VMEM((14, 32, 128), f32),
+            pltpu.VMEM((4, 32, 128), f32),
+            pltpu.VMEM((14, 32, 128), f32),
             pltpu.VMEM((4, 32, 128), f32),
             pltpu.VMEM((14, 32, 128), f32),
             pltpu.SemaphoreType.DMA((N_COPIES,)),

time: 134 us -> 99.3 us (0.74)
  Pallas kernels: 128 us -> 94.7 us
    pallas_call x1, Pallas kernels: 128 us -> 94.7 us  [body(): pl.pallas_call(kernel, out_shape=(jax.ShapeDtypeStruct((1, Q, B), f32),)...]
where the time goes in v2:
time: 99.3 us; the launch traced here: 99.1 us
  Pallas kernels  94.7 us (95%)
  local copies, waits for them, and re-layouts  3.18 us (3%)
  between operations  1.29 us (1%)
    pallas_call x1, Pallas kernels, body(): pl.pallas_call(kernel, out_shape=(jax.ShapeDtypeStruct((1, Q, B), f32),)...  94.7 us
    unnamed x2, local copies, waits for them, and re-layouts  3.18 us

profile of v2, /device:TPU:8, one launch (start us, length us, event | category | flops | bytes accessed | tf_op | source)
XLA Modules:
  0.0 99.1 jit_solution(17555885917714014429)
XLA Ops:
  1.3 94.7 %block_cg.1 = (f32[1,64,576]{2,1,0:T(8,128)}, f32[1,64,576]{2,1,0:T(8,128)}) custom-call(s32[1,1,16]{2,1,0:T(1,128)} %rows_ref.1, s32[1,1,16]{2,1,0:T(1,128)} %cols_ref.1, s32[1,1]{1,0:T(1,128)S(6)} %copy.10.counts_ref, bf16[1,1,16,576,576]{4,3,2,1,0:T(8,128)(2,1)} %tiles_ref.1, bf16[1,576,576]{2,1,0:T(8,128)(2,1)} %diag_ref.1, f32[1,64,576]{2,1,0:T(8,128)} %probes_ref.1), custom_call_target="tpu_custom_call" | custom-call | tf_op jit(solution)/shard_map/block_cg/pallas_call | solution.py:506
  95.9 1.6 %copy.11 = f32[1,64,576]{2,1,0:T(8,128)} copy(f32[1,64,576]{2,1,0:T(8,128)} %get-tuple-element.4) | data formatting | bytes 294912
  97.5 1.6 %copy.12 = f32[1,64,576]{2,1,0:T(8,128)} copy(f32[1,64,576]{2,1,0:T(8,128)} %get-tuple-element.5) | data formatting | bytes 294912

commit v3 on v2

--- a/solution.py
+++ b/solution.py
@@ -1,3 +1,5 @@
+import math
+
 import jax
 import jax.numpy as jnp
 from jax import lax
@@ -9,7 +11,9 @@
 B, Q, SLOTS, ROWS, PLANE = 576, 64, 16, 8, 32
 PK, HALF = 288, 144
 STEPS = (1, 3, 2)
-N_COPIES = 248
+ORDER = (2, 1, 3, 0)
+N_ARRIVALS = 92
+SENT = 26000
 NT = 256
 UNROLL = 4
 
@@ -91,7 +95,7 @@
 def kernel(
     rows_ref, cols_ref, counts_ref, tiles_ref, diag_ref, probes_ref,
     sol_ref, res_ref,
-    blocks, diag, rp_a, rp_b, cp_a, cp_b, ps, xb, qb, r1, sb, r2, pz, zq, zr1, zh, zr2,
+    blocks, diag, rp_a, rp_b, cp_a, cp_b, ps, xb, qb, r1, sb, r2, pz, zq, zin, zr2, gone,
     seg_r, seg_c, prev_r, prev_c, last_r, last_c,
     ar_a, ar_ar, ar_b, ar_br, ar_c, ar_cr, ar_d, ar_dr,
     send_sem, recv_sem, tile_sem, diag_sem,
@@ -111,21 +115,38 @@
         return lax.rem(v + 2 * n, n)
 
     plane_of = {0: lambda d: at(dx=d), 1: lambda d: at(dy=d)}
-    used = []
     rps, cps = (rp_a, rp_b), (cp_a, cp_b)
-
-    def send(src, dst, device):
-        i = len(used)
-        copy = pltpu.make_async_remote_copy(
-            src_ref=src, dst_ref=dst, send_sem=send_sem.at[i], recv_sem=recv_sem.at[i],
+    arrivals = [0]
+    sent = [0, 0]
+    turn = [0]
+
+    def group():
+        arrivals[0] += 1
+        return arrivals[0] - 1
+
+    def send(src, dst, device, g):
+        pltpu.make_async_remote_copy(
+            src_ref=src, dst_ref=dst, send_sem=send_sem.at[turn[0]], recv_sem=recv_sem.at[g],
             device_id=device, device_id_type=MESH,
-        )
-        used.append(copy)
-        copy.start()
-        return copy
+        ).start()
+        width = 1 if src.dtype == jnp.bfloat16 else 2
+        sent[turn[0]] += width * math.prod(src.shape) // 128
+
+    def take(g, ref):
+        pltpu.make_async_remote_copy(
+            src_ref=ref, dst_ref=ref, send_sem=send_sem.at[0], recv_sem=recv_sem.at[g],
+            device_id=at(flip=True), device_id_type=MESH,
+        ).wait_recv()
+
+    def drain(p):
+        ref = gone.at[pl.ds(0, sent[p])]
+        pltpu.make_async_remote_copy(
+            src_ref=ref, dst_ref=ref, send_sem=send_sem.at[p], recv_sem=recv_sem.at[0],
+            device_id=at(flip=True), device_id_type=MESH,
+        ).wait_send()
 
     tile_copies = [
-        pltpu.make_async_copy(tiles_ref.at[0, 0, s], blocks.at[s], tile_sem.at[s])
+        pltpu.make_async_copy(tiles_ref.at[0, 0, s], blocks.at[s], tile_sem.at[0])
         for s in range(SLOTS)
     ]
     diag_copy = pltpu.make_async_copy(diag_ref.at[0], diag, diag_sem.at[0])
@@ -143,59 +164,61 @@
     def gather_begin(p, value):
         rps[p][k, y, x] = value
         cps[p][z] = value
-        first, second, far = [], [], []
-        for h in range(2):
-            own = rps[p].at[k, y, x, half(h)]
-            first.append([send(own, own, plane_of[h](d)) for d in STEPS])
+        first = [[group() for _ in STEPS] for _ in range(2)]
+        second = [[group() for _ in STEPS] for _ in range(2)]
+        far, rest, across = [group(), group()], group(), group()
         own = cps[p].at[z]
-        for d in (2, -2, 1, -1):
-            far.append(send(own, own, at(dz=d)))
-        for h in range(2):
-            own = rps[p].at[k, y, x, half(h)]
-            second.append([[send(own, own, plane_of[1 - h](e)) for e in STEPS]])
-        return first, second, far
-
-    def gather_forward(p, state):
-        first, second, far = state
+        for d, g in ((2, far[0]), (-2, far[1])):
+            send(own, own, at(dz=d), g)
         for i, d in enumerate(STEPS):
             for h in range(2):
-                first[h][i].wait_recv()
+                own = rps[p].at[k, y, x, half(h)]
+                send(own, own, plane_of[h](d), first[h][i])
+        own = cps[p].at[z]
+        for d in (1, -1):
+            send(own, own, at(dz=d), rest)
+        for j, e in enumerate(STEPS):
+            for h in range(2):
+                own = rps[p].at[k, y, x, half(h)]
+                send(own, own, plane_of[1 - h](e), second[h][j])
+        return first, second, far, rest, across
+
+    def gather_forward(p, state):
+        first, second, far, rest, across = state
+        for i, d in enumerate(STEPS):
+            for h in range(2):
                 ty, tx = (y, wrap(x - d, 4)) if h == 0 else (wrap(y - d, 4), x)
                 got = rps[p].at[k, ty, tx, half(h)]
-                second[h].append([send(got, got, plane_of[1 - h](e)) for e in STEPS])
+                take(first[h][i], got)
+                for j, e in enumerate(STEPS):
+                    send(got, got, plane_of[1 - h](e), second[h][j])
         for i, d in enumerate((2, -2)):
-            far[i].wait_recv()
             got = cps[p].at[wrap(z - d, 8)]
-            far.append(send(got, got, at(dz=d // 2)))
+            take(far[i], got)
+            send(got, got, at(dz=d // 2), rest)
             got = cps[p].at[wrap(z - d, 8), half(i)]
-            far.append(send(got, got, at(dz=d)))
-        third = []
+            send(got, got, at(dz=d), rest)
         for h in range(2):
-            group = rps[p].at[k, y, :, half(h)] if h == 0 else rps[p].at[k, :, x, half(h)]
-            third.append(send(group, group, at(flip=True)))
-        return first, second, far, third
+            line = rps[p].at[k, y, :, half(h)] if h == 0 else rps[p].at[k, :, x, half(h)]
+            send(line, line, at(flip=True), across)
 
     def gather_across(p, state):
-        first, second, far, third = state
+        first, second, far, rest, across = state
         for j, e in enumerate(STEPS):
             for h in range(2):
-                for part in second[h]:
-                    part[j].wait_recv()
-                group = (
+                line = (
                     rps[p].at[k, wrap(y - e, 4), :, half(h)]
                     if h == 0
                     else rps[p].at[k, :, wrap(x - e, 4), half(h)]
                 )
-                third.append(send(group, group, at(flip=True)))
-
-    def gather_end_z(state):
-        far = state[2]
-        for copy in far[2:]:
-            copy.wait_recv()
-
-    def gather_end_plane(state):
-        for copy in state[3]:
-            copy.wait_recv()
+                take(second[h][j], line)
+                send(line, line, at(flip=True), across)
+
+    def gather_end_z(p, state):
+        take(state[3], cps[p].at[pl.ds(0, 5)])
+
+    def gather_end_plane(p, state):
+        take(state[4], rps[p].at[1 - k])
 
     def forward_products(p):
         def step(s, carry):
@@ -205,7 +228,7 @@
 
         lax.fori_loop(0, SLOTS, step, 0, unroll=UNROLL)
 
-    def mirror_products(p):
+    def mirror_products(p, low, high, cross):
         count = counts_ref[0, 0]
 
         def step(s, cross):
@@ -217,8 +240,7 @@
             held = jnp.where(s < count, 1.0, 0.0)
             return cross + held * dot(far, product.astype(jnp.bfloat16), 1, 1)
 
-        cross = lax.fori_loop(0, SLOTS, step, jnp.zeros((Q, Q), jnp.float32), unroll=UNROLL)
-        return cross + cross.T
+        return lax.fori_loop(low, high, step, cross, unroll=UNROLL)
 
     def plane_begin(p):
         def fill(kk):
@@ -227,62 +249,64 @@
                 ps[p, kk, t // 4, lax.rem(t, 4)] = seg_r[last_r[2 * t + kk]].astype(jnp.bfloat16)
 
         fill(1 - k)
-        out = []
-        for d in (2, 1, 3, 0):
+        across = {}
+        for d in ORDER:
             for h in range(2):
+                across[h, d] = group()
                 if h == 0:
                     t = wrap(x + d, 4)
                     src, dst = ps.at[p, 1 - k, :, t, half(h)], xb.at[p, :, t, half(h)]
                 else:
                     t = wrap(y + d, 4)
                     src, dst = ps.at[p, 1 - k, t, :, half(h)], xb.at[p, t, :, half(h)]
-                out.append(send(src, dst, at(flip=True)))
+                send(src, dst, at(flip=True), across[h, d])
         fill(k)
+        return across
+
+    def plane_stage(p, across, d):
+        out = []
+        for h in range(2):
+            if h == 0:
+                t, mine = wrap(x + d, 4), y
+                take(across[h, d], xb.at[p, :, t, half(h)])
+                total = ps[p, k, :, t, half(h)].astype(jnp.float32) + xb[p, :, t, half(h)].astype(jnp.float32)
+            else:
+                t, mine = wrap(y + d, 4), x
+                take(across[h, d], xb.at[p, t, :, half(h)])
+                total = ps[p, k, t, :, half(h)].astype(jnp.float32) + xb[p, t, :, half(h)].astype(jnp.float32)
+            qb[p, h, d] = total.astype(jnp.bfloat16)
+            g = group()
+            for e in (2, 1, 3):
+                send(qb.at[p, h, d, wrap(mine + e, 4)], r1.at[p, h, d, e - 1], plane_of[1 - h](e), g)
+            out.append(g)
         return out
 
-    def plane_stage(p, across):
-        out = [{}, {}]
-        n = 0
-        for d in (2, 1, 3, 0):
+    def plane_stage2(p, mid, hooks):
+        last = group()
+        own = []
+        for d in ORDER:
             for h in range(2):
-                across[n].wait_recv()
-                n += 1
-                if h == 0:
-                    t, mine = wrap(x + d, 4), y
-                    total = ps[p, k, :, t, half(h)].astype(jnp.float32) + xb[p, :, t, half(h)].astype(jnp.float32)
-                else:
-                    t, mine = wrap(y + d, 4), x
-                    total = ps[p, k, t, :, half(h)].astype(jnp.float32) + xb[p, t, :, half(h)].astype(jnp.float32)
-                qb[p, h, d] = total.astype(jnp.bfloat16)
-                out[h][d] = [
-                    send(qb.at[p, h, d, wrap(mine + e, 4)], r1.at[p, h, d, e - 1], plane_of[1 - h](e))
-                    for e in (2, 1, 3)
-                ]
-        return out
-
-    def plane_stage2(p, mid):
-        out = [[], []]
-        for d in (2, 1, 3, 0):
-            for h in range(2):
-                for copy in mid[h][d]:
-                    copy.wait_recv()
+                take(mid[d][h], r1.at[p, h, d])
                 total = qb[p, h, d, y if h == 0 else x].astype(jnp.float32)
                 for e in range(3):
                     total = total + r1[p, h, d, e].astype(jnp.float32)
                 if d != 0:
                     sb[p, h, d] = total.astype(jnp.bfloat16)
-                    out[h].append(send(sb.at[p, h, d], r2.at[p, h, d - 1], plane_of[h](d)))
+                    send(sb.at[p, h, d], r2.at[p, h, d - 1], plane_of[h](d), last)
                 else:
-                    out[h].append(total)
-        return out
-
-    def plane_end(p, last):
+                    own.append(total)
+            if d in hooks:
+                hooks[d]()
+        return last, own
+
+    def plane_end(p, state):
+        last, own = state
+        take(last, r2.at[p])
         halves = []
         for h in range(2):
-            total = last[h][3]
-            for i, d in enumerate((2, 1, 3)):
-                last[h][i].wait_recv()
-                total = total + r2[p, h, d - 1].astype(jnp.float32)
+            total = own[h]
+            for d in range(3):
+                total = total + r2[p, h, d].astype(jnp.float32)
             halves.append(total)
         return jnp.concatenate(halves, axis=0)
 
@@ -291,22 +315,20 @@
         def _(t):
             pz[p, t] = seg_c[last_c[t]].astype(jnp.bfloat16)
 
-        out = [
-            send(pz.at[p, wrap(z + 3, 8)], zr1.at[p, 0], at(dz=1)),
-            send(pz.at[p, wrap(z - 3, 8)], zr1.at[p, 1], at(dz=-1)),
-            send(pz.at[p, wrap(z + 4, 8), half(0)], zh.at[p, 0], at(dz=2)),
-            send(pz.at[p, wrap(z + 4, 8), half(1)], zh.at[p, 1], at(dz=-2)),
-            send(pz.at[p, wrap(z + 1, 8)], zr2.at[p, 0], at(dz=1)),
-            send(pz.at[p, wrap(z - 1, 8)], zr2.at[p, 1], at(dz=-1)),
-        ]
-        return out
-
-    def z_stage(p, out):
+        near, far = [group(), group()], group()
+        for i, d in enumerate((1, -1)):
+            send(pz.at[p, wrap(z + 3 * d, 8)], zin.at[p, i, pl.ds(0, PK)], at(dz=d), near[i])
+            send(pz.at[p, wrap(z + 4, 8), half(i)], zin.at[p, i, pl.ds(PK, HALF)], at(dz=2 * d), near[i])
+        for i, d in enumerate((1, -1)):
+            send(pz.at[p, wrap(z + d, 8)], zr2.at[p, i], at(dz=d), far)
+        return near, far
+
+    def z_stage(p, state):
+        near, far = state
         for i, d in enumerate((2, -2)):
-            out[i].wait_recv()
-            out[2 + i].wait_recv()
-            total = pz[p, wrap(z + d, 8)].astype(jnp.float32) + zr1[p, i].astype(jnp.float32)
-            extra = zh[p, i].astype(jnp.float32)
+            take(near[i], zin.at[p, i])
+            total = pz[p, wrap(z + d, 8)].astype(jnp.float32) + zin[p, i, 0:PK].astype(jnp.float32)
+            extra = zin[p, i, PK : PK + HALF].astype(jnp.float32)
             lo, hi = total[0:HALF], total[HALF:PK]
             if i == 0:
                 lo = lo + extra
@@ -314,12 +336,12 @@
                 hi = hi + extra
             zq[p, i, 0:HALF] = lo.astype(jnp.bfloat16)
             zq[p, i, HALF:PK] = hi.astype(jnp.bfloat16)
-            out.append(send(zq.at[p, i], zr2.at[p, 2 + i], at(dz=d)))
-
-    def z_end(p, out):
+            send(zq.at[p, i], zr2.at[p, 2 + i], at(dz=d), far)
+
+    def z_end(p, state):
+        take(state[1], zr2.at[p])
         total = pz[p, z].astype(jnp.float32)
         for i in range(4):
-            out[4 + i].wait_recv()
             total = total + zr2[p, i].astype(jnp.float32)
         return total
 
@@ -332,27 +354,20 @@
     bases = (0, 1, 4, 7)
 
     def reduce_steps(buf, rbuf, value):
-        buf[0, 0 : value.shape[0]] = value
+        buf[0] = value
         for stage in range(4):
-            copies = [
-                send(buf.at[stage], rbuf.at[bases[stage] + i], peer)
-                for i, peer in enumerate(groups[stage])
-            ]
+            g = group()
+            for i, peer in enumerate(groups[stage]):
+                send(buf.at[stage], rbuf.at[bases[stage] + i], peer, g)
             yield None
             total = buf[stage]
-            for i, copy in enumerate(copies):
-                copy.wait_recv()
+            n = len(groups[stage])
+            take(g, rbuf.at[pl.ds(bases[stage], n)])
+            for i in range(n):
                 total = total + rbuf[bases[stage] + i]
             if stage < 3:
                 buf[stage + 1] = total
         yield total
-
-    drained = [0]
-
-    def drain():
-        for copy in used[drained[0] :]:
-            copy.wait_send()
-        drained[0] = len(used)
 
     def own_product(v):
         hi = v.astype(jnp.bfloat16)
@@ -405,63 +420,76 @@
         ar_a, ar_ar, jnp.concatenate([fold(g00), jnp.broadcast_to(trace, (8, 128))], axis=0)
     )
     next(red_a)
-    state = gather_forward(0, state)
+    gather_forward(0, state)
     for copy in tile_copies[8:]:
         copy.start()
     next(red_a)
     own = own_product(probes)
     gather_across(0, state)
     next(red_a)
-    gather_end_z(state)
-    for copy in tile_copies:
-        copy.wait()
+    gather_end_z(0, state)
+    pltpu.make_async_copy(tiles_ref.at[0, 0], blocks, tile_sem.at[0]).wait()
     forward_products(0)
     across = plane_begin(0)
     next(red_a)
-    gather_end_plane(state)
-    cross = mirror_products(0)
+    gather_end_plane(0, state)
+    mid = {}
+    cross = mirror_products(0, 0, 8, jnp.zeros((Q, Q), jnp.float32))
+    mid[2] = plane_stage(0, across, 2)
+    cross = mirror_products(0, 8, 12, cross)
+    mid[1] = plane_stage(0, across, 1)
+    cross = mirror_products(0, 12, 16, cross)
+    cross = cross + cross.T
     zs = z_begin(0)
+    mid[3] = plane_stage(0, across, 3)
+    mid[0] = plane_stage(0, across, 0)
     red_b = reduce_steps(ar_b, ar_br, fold(gram(probes, own) + cross))
     next(red_b)
-    mid = plane_stage(0, across)
     total = next(red_a)
     rr0 = unfold(total[0:32])
     shift = total[32:33, 0:1] * (1.0 / (NT * B))
-    z_stage(0, zs)
-    next(red_b)
     eye = (
         lax.broadcasted_iota(jnp.int32, (Q, Q), 0) == lax.broadcasted_iota(jnp.int32, (Q, Q), 1)
     ).astype(jnp.float32)
     rr0_inv = solve(rr0, eye)
-    last = plane_stage2(0, mid)
     next(red_b)
+    z_stage(0, zs)
+    last = plane_stage2(0, mid, {2: lambda: next(red_b), 3: lambda: next(red_b)})
     image = z_end(0, zs)
     image = image + plane_end(0, last)
     image = own + unpack(image)
     basis = image - shift * probes
 
+    turn[0] = 1
     state = gather_begin(1, pack(basis).astype(jnp.bfloat16))
-    next(red_b)
     red_c = reduce_steps(ar_c, ar_cr, fold(gram(basis, basis)))
     next(red_c)
     own = own_product(basis)
-    state = gather_forward(1, state)
+    gather_forward(1, state)
     next(red_c)
     pq0 = unfold(next(red_b))
     alpha = solve(pq0, rr0)
-    drain()
+    drain(0)
     gather_across(1, state)
     next(red_c)
-    gather_end_z(state)
+    gather_end_z(1, state)
     forward_products(1)
     across = plane_begin(1)
     next(red_c)
-    gather_end_plane(state)
-    cross = mirror_products(1)
+    gather_end_plane(1, state)
+    mid = {}
+    cross = mirror_products(1, 0, 8, jnp.zeros((Q, Q), jnp.float32))
+    mid[2] = plane_stage(1, across, 2)
+    cross = mirror_products(1, 8, 12, cross)
+    mid[1] = plane_stage(1, across, 1)
+    cross = mirror_products(1, 12, 16, cross)
+    cross = cross + cross.T
     zs = z_begin(1)
     red_d = reduce_steps(ar_d, ar_dr, fold(gram(basis, own) + cross))
     next(red_d)
-    mid = plane_stage(1, across)
+    mid[3] = plane_stage(1, across, 3)
+    mid[0] = plane_stage(1, across, 0)
+    next(red_d)
     g11 = unfold(next(red_c))
     g01 = pq0 - shift * rr0
     m0 = eye - shift * alpha
@@ -472,16 +500,15 @@
     )
     beta = dot_hi(rr0_inv, rr1, 1, 0)
     n0 = m0 + beta
+    residual = combine(m0, probes) + combine(m1, basis)
+    next(red_d)
     z_stage(1, zs)
-    next(red_d)
-    residual = combine(m0, probes) + combine(m1, basis)
     direction = residual + combine(beta, probes)
     xsol = combine(alpha, probes)
     partial = combine(n0, image)
-    next(red_d)
-    last = plane_stage2(1, mid)
-    next(red_d)
-    g12 = unfold(next(red_d))
+    final = []
+    last = plane_stage2(1, mid, {2: lambda: next(red_d), 0: lambda: final.append(next(red_d))})
+    g12 = unfold(final[0])
     g02 = g11 + shift * g01
     pq1 = (
         dot_hi(n0, dot_hi(pq0, n0, 1, 0) + dot_hi(g02, m1, 1, 0), 0, 0)
@@ -495,7 +522,7 @@
     deep = deep + plane_end(1, last)
     deep = own + unpack(deep)
     res_ref[0] = start - combine(m2, deep)
-    drain()
+    drain(1)
 
 
 def body(tiles, diag_tiles, probes, rows_list, cols_list, counts):
@@ -523,9 +550,9 @@
             pltpu.VMEM((2, 2, 3, HALF, 128), bf),
             pltpu.VMEM((2, ROWS, PK, 128), bf),
             pltpu.VMEM((2, 2, PK, 128), bf),
-            pltpu.VMEM((2, 2, PK, 128), bf),
-            pltpu.VMEM((2, 2, HALF, 128), bf),
+            pltpu.VMEM((2, 2, PK + HALF, 128), bf),
             pltpu.VMEM((2, 4, PK, 128), bf),
+            pltpu.VMEM((SENT, 128), bf),
             pltpu.VMEM((SLOTS + 1, PK, 128), f32),
             pltpu.VMEM((SLOTS + 1, PK, 128), f32),
             pltpu.SMEM((SLOTS,), i32),
@@ -540,9 +567,9 @@
             pltpu.VMEM((14, 32, 128), f32),
             pltpu.VMEM((4, 32, 128), f32),
             pltpu.VMEM((14, 32, 128), f32),
-            pltpu.SemaphoreType.DMA((N_COPIES,)),
-            pltpu.SemaphoreType.DMA((N_COPIES,)),
-            pltpu.SemaphoreType.DMA((SLOTS,)),
+            pltpu.SemaphoreType.DMA((2,)),
+            pltpu.SemaphoreType.DMA((N_ARRIVALS,)),
+            pltpu.SemaphoreType.DMA((1,)),
             pltpu.SemaphoreType.DMA((1,)),
         ],
         compiler_params=pltpu.CompilerParams(

time: 99.3 us -> 90.6 us (0.912)
  Pallas kernels: 94.7 us -> 86 us
    pallas_call x1, Pallas kernels: 94.7 us -> 86 us  [body(): pl.pallas_call(kernel, out_shape=(jax.ShapeDtypeStruct((1, Q, B), f32),)...]
where the time goes in v3:
time: 90.6 us; the launch traced here: 90.5 us
  Pallas kernels  86 us (95%)
  local copies, waits for them, and re-layouts  3.18 us (4%)
  between operations  1.29 us (1%)
    pallas_call x1, Pallas kernels, body(): pl.pallas_call(kernel, out_shape=(jax.ShapeDtypeStruct((1, Q, B), f32),)...  86 us
    unnamed x2, local copies, waits for them, and re-layouts  3.18 us

profile of v3, /device:TPU:8, one launch (start us, length us, event | category | flops | bytes accessed | tf_op | source)
XLA Modules:
  0.0 90.5 jit_solution(2758876425386176082)
XLA Ops:
  1.3 86.0 %block_cg.1 = (f32[1,64,576]{2,1,0:T(8,128)}, f32[1,64,576]{2,1,0:T(8,128)}) custom-call(s32[1,1,16]{2,1,0:T(1,128)} %rows_ref.1, s32[1,1,16]{2,1,0:T(1,128)} %cols_ref.1, s32[1,1]{1,0:T(1,128)S(6)} %copy.10.counts_ref, bf16[1,1,16,576,576]{4,3,2,1,0:T(8,128)(2,1)} %tiles_ref.1, bf16[1,576,576]{2,1,0:T(8,128)(2,1)} %diag_ref.1, f32[1,64,576]{2,1,0:T(8,128)} %probes_ref.1), custom_call_target="tpu_custom_call" | custom-call | tf_op jit(solution)/shard_map/block_cg/pallas_call | solution.py:533
  87.3 1.6 %copy.11 = f32[1,64,576]{2,1,0:T(8,128)} copy(f32[1,64,576]{2,1,0:T(8,128)} %get-tuple-element.4) | data formatting | bytes 294912
  88.9 1.6 %copy.12 = f32[1,64,576]{2,1,0:T(8,128)} copy(f32[1,64,576]{2,1,0:T(8,128)} %get-tuple-element.5) | data formatting | bytes 294912

commit v4 on v3

--- a/solution.py
+++ b/solution.py
@@ -96,7 +96,7 @@
     rows_ref, cols_ref, counts_ref, tiles_ref, diag_ref, probes_ref,
     sol_ref, res_ref,
     blocks, diag, rp_a, rp_b, cp_a, cp_b, ps, xb, qb, r1, sb, r2, pz, zq, zin, zr2, gone,
-    seg_r, seg_c, prev_r, prev_c, last_r, last_c,
+    kept, seg_r, seg_c, prev_r, prev_c, last_r, last_c,
     ar_a, ar_ar, ar_b, ar_br, ar_c, ar_cr, ar_d, ar_dr,
     send_sem, recv_sem, tile_sem, diag_sem,
 ):
@@ -234,13 +234,26 @@
         def step(s, cross):
             t = rows_ref[0, 0, s]
             near = unpack(rps[p][lax.rem(t, 2), t // 8, lax.rem(t // 2, 4)])
-            far = unpack(cps[p][cols_ref[0, 0, s]])
             product = dot(near, blocks[s], 1, 0)
             seg_c[s] = pack(product) + seg_c[prev_c[s]]
+            if p == 0:
+                kept[s] = product.astype(jnp.bfloat16)
+                return cross
+            far = unpack(cps[p][cols_ref[0, 0, s]])
             held = jnp.where(s < count, 1.0, 0.0)
             return cross + held * dot(far, product.astype(jnp.bfloat16), 1, 1)
 
         return lax.fori_loop(low, high, step, cross, unroll=UNROLL)
+
+    def late_cross(p, cross):
+        count = counts_ref[0, 0]
+
+        def step(s, cross):
+            far = unpack(cps[p][cols_ref[0, 0, s]])
+            held = jnp.where(s < count, 1.0, 0.0)
+            return cross + held * dot(far, kept[s], 1, 1)
+
+        return lax.fori_loop(0, SLOTS, step, cross, unroll=UNROLL)
 
     def plane_begin(p):
         def fill(kk):
@@ -439,10 +452,11 @@
     cross = mirror_products(0, 8, 12, cross)
     mid[1] = plane_stage(0, across, 1)
     cross = mirror_products(0, 12, 16, cross)
-    cross = cross + cross.T
     zs = z_begin(0)
     mid[3] = plane_stage(0, across, 3)
     mid[0] = plane_stage(0, across, 0)
+    cross = late_cross(0, cross)
+    cross = cross + cross.T
     red_b = reduce_steps(ar_b, ar_br, fold(gram(probes, own) + cross))
     next(red_b)
     total = next(red_a)
@@ -451,17 +465,24 @@
     eye = (
         lax.broadcasted_iota(jnp.int32, (Q, Q), 0) == lax.broadcasted_iota(jnp.int32, (Q, Q), 1)
     ).astype(jnp.float32)
-    rr0_inv = solve(rr0, eye)
+    offset = pack(own - shift * probes)
     next(red_b)
     z_stage(0, zs)
-    last = plane_stage2(0, mid, {2: lambda: next(red_b), 3: lambda: next(red_b)})
-    image = z_end(0, zs)
-    image = image + plane_end(0, last)
-    image = own + unpack(image)
-    basis = image - shift * probes
+    inverse = []
+
+    def after_sends():
+        next(red_b)
+        inverse.append(solve(rr0, eye))
+
+    last = plane_stage2(0, mid, {2: lambda: next(red_b), 3: after_sends})
+    rr0_inv = inverse[0]
+    packed = offset + z_end(0, zs)
+    packed = packed + plane_end(0, last)
 
     turn[0] = 1
-    state = gather_begin(1, pack(basis).astype(jnp.bfloat16))
+    state = gather_begin(1, packed.astype(jnp.bfloat16))
+    basis = unpack(packed)
+    image = basis + shift * probes
     red_c = reduce_steps(ar_c, ar_cr, fold(gram(basis, basis)))
     next(red_c)
     own = own_product(basis)
@@ -503,26 +524,33 @@
     residual = combine(m0, probes) + combine(m1, basis)
     next(red_d)
     z_stage(1, zs)
+    next(red_d)
     direction = residual + combine(beta, probes)
     xsol = combine(alpha, probes)
     partial = combine(n0, image)
-    final = []
-    last = plane_stage2(1, mid, {2: lambda: next(red_d), 0: lambda: final.append(next(red_d))})
-    g12 = unfold(final[0])
     g02 = g11 + shift * g01
-    pq1 = (
-        dot_hi(n0, dot_hi(pq0, n0, 1, 0) + dot_hi(g02, m1, 1, 0), 0, 0)
-        + dot_hi(m1, dot_hi(g02, n0, 0, 0) + dot_hi(g12, m1, 1, 0), 0, 0)
-    )
-    gamma = solve(pq1, rr1)
-    sol_ref[0] = xsol + combine(gamma, direction)
-    start = residual - combine(gamma, partial)
-    m2 = dot_hi(m1, gamma, 1, 0)
+    known = dot_hi(n0, dot_hi(pq0, n0, 1, 0) + dot_hi(g02, m1, 1, 0), 0, 0) + dot_hi(
+        m1, dot_hi(g02, n0, 0, 0), 0, 0
+    )
+    found = []
+
+    def finish():
+        g12 = unfold(next(red_d))
+        found.append(solve(known + dot_hi(m1, dot_hi(g12, m1, 1, 0), 0, 0), rr1))
+
+    last = plane_stage2(1, mid, {3: finish})
+    drain(1)
+    gamma = found[0]
     deep = z_end(1, zs)
     deep = deep + plane_end(1, last)
-    deep = own + unpack(deep)
-    res_ref[0] = start - combine(m2, deep)
-    drain(1)
+    image2 = partial + combine(m1, own + unpack(deep))
+    sol_ref[...] = xsol + combine(gamma, direction)
+    res_ref[...] = residual - combine(gamma, image2)
+
+
+def close(sol_ref, res_ref, sol_out, res_out):
+    sol_out[0] = sol_ref[...]
+    res_out[0] = res_ref[...]
 
 
 def body(tiles, diag_tiles, probes, rows_list, cols_list, counts):
@@ -530,9 +558,10 @@
     vmem = pl.BlockSpec(memory_space=pltpu.VMEM)
     hbm = pl.BlockSpec(memory_space=pl.ANY)
     bf, f32, i32 = jnp.bfloat16, jnp.float32, jnp.int32
-    return pl.pallas_call(
+    wide = jax.ShapeDtypeStruct((Q, B), f32)
+    parts = pl.pallas_call(
         kernel,
-        out_shape=(jax.ShapeDtypeStruct((1, Q, B), f32),) * 2,
+        out_shape=(wide, wide),
         in_specs=[smem, smem, smem, hbm, hbm, vmem],
         out_specs=(vmem, vmem),
         scratch_shapes=[
@@ -553,6 +582,7 @@
             pltpu.VMEM((2, 2, PK + HALF, 128), bf),
             pltpu.VMEM((2, 4, PK, 128), bf),
             pltpu.VMEM((SENT, 128), bf),
+            pltpu.VMEM((SLOTS, Q, B), bf),
             pltpu.VMEM((SLOTS + 1, PK, 128), f32),
             pltpu.VMEM((SLOTS + 1, PK, 128), f32),
             pltpu.SMEM((SLOTS,), i32),
@@ -577,6 +607,13 @@
         ),
         name="block_cg",
     )(rows_list, cols_list, counts, tiles, diag_tiles, probes)
+    return pl.pallas_call(
+        close,
+        out_shape=(jax.ShapeDtypeStruct((1, Q, B), f32),) * 2,
+        in_specs=[vmem] * 2,
+        out_specs=(vmem, vmem),
+        name="close",
+    )(*parts)
 
 
 def solution(mesh):

time: 90.6 us -> 89.7 us (0.990)
  local copies, waits for them, and re-layouts: 3.18 us -> 0 us
  Pallas kernels: 86 us -> 88.2 us
    unnamed x2 -> x0, local copies, waits for them, and re-layouts: 3.18 us -> none
    pallas_call x1 -> x2, Pallas kernels: 86 us -> 88.2 us  [the longest x1 86.5 us: body(): pl.pallas_call(kernel, out_shape=(wide, wide), in_specs=[smem, smem, smem...]
where the time goes in v4:
time: 89.7 us; the launch traced here: 89.5 us
  Pallas kernels  88.2 us (98%)
  between operations  1.29 us (1%)
    pallas_call x1, Pallas kernels, body(): pl.pallas_call(kernel, out_shape=(wide, wide), in_specs=[smem, smem, smem...  86.5 us

profile of v4, /device:TPU:8, one launch (start us, length us, event | category | flops | bytes accessed | tf_op | source)
XLA Modules:
  0.0 89.5 jit_solution(11012388620672479312)
XLA Ops:
  1.3 86.5 %block_cg.1 = (f32[64,576]{1,0:T(8,128)}, f32[64,576]{1,0:T(8,128)}) custom-call(s32[1,1,16]{2,1,0:T(1,128)} %rows_ref.1, s32[1,1,16]{2,1,0:T(1,128)} %cols_ref.1, s32[1,1]{1,0:T(1,128)S(6)} %copy.8.counts_ref, bf16[1,1,16,576,576]{4,3,2,1,0:T(8,128)(2,1)} %tiles_ref.1, bf16[1,576,576]{2,1,0:T(8,128)(2,1)} %diag_ref.1, f32[1,64,576]{2,1,0:T(8,128)} %probes_ref.1), custom_call_target="tpu_custom_call" | custom-call | tf_op jit(solution)/shard_map/block_cg/pallas_call | solution.py:562
  87.8 1.7 %close.1 = (f32[1,64,576]{2,1,0:T(8,128)}, f32[1,64,576]{2,1,0:T(8,128)}) custom-call(f32[64,576]{1,0:T(8,128)} %get-tuple-element.4.sol_ref, f32[64,576]{1,0:T(8,128)} %get-tuple-element.5.res_ref), custom_call_target="tpu_custom_call" | custom-call | tf_op jit(solution)/shard_map/close/pallas_call | solution.py:610

commit v5 on v4

--- a/solution.py
+++ b/solution.py
@@ -257,7 +257,7 @@
 
     def plane_begin(p):
         def fill(kk):
-            @pl.loop(0, 16)
+            @pl.loop(0, 16, unroll=4)
             def _(t):
                 ps[p, kk, t // 4, lax.rem(t, 4)] = seg_r[last_r[2 * t + kk]].astype(jnp.bfloat16)
 
@@ -324,7 +324,7 @@
         return jnp.concatenate(halves, axis=0)
 
     def z_begin(p):
-        @pl.loop(0, ROWS)
+        @pl.loop(0, ROWS, unroll=4)
         def _(t):
             pz[p, t] = seg_c[last_c[t]].astype(jnp.bfloat16)
 
@@ -468,14 +468,7 @@
     offset = pack(own - shift * probes)
     next(red_b)
     z_stage(0, zs)
-    inverse = []
-
-    def after_sends():
-        next(red_b)
-        inverse.append(solve(rr0, eye))
-
-    last = plane_stage2(0, mid, {2: lambda: next(red_b), 3: after_sends})
-    rr0_inv = inverse[0]
+    last = plane_stage2(0, mid, {1: lambda: next(red_b), 3: lambda: next(red_b)})
     packed = offset + z_end(0, zs)
     packed = packed + plane_end(0, last)
 
@@ -485,9 +478,10 @@
     image = basis + shift * probes
     red_c = reduce_steps(ar_c, ar_cr, fold(gram(basis, basis)))
     next(red_c)
-    own = own_product(basis)
+    rr0_inv = solve(rr0, eye)
     gather_forward(1, state)
     next(red_c)
+    own = own_product(basis)
     pq0 = unfold(next(red_b))
     alpha = solve(pq0, rr0)
     drain(0)
@@ -521,29 +515,30 @@
     )
     beta = dot_hi(rr0_inv, rr1, 1, 0)
     n0 = m0 + beta
-    residual = combine(m0, probes) + combine(m1, basis)
     next(red_d)
-    z_stage(1, zs)
-    next(red_d)
-    direction = residual + combine(beta, probes)
-    xsol = combine(alpha, probes)
-    partial = combine(n0, image)
     g02 = g11 + shift * g01
     known = dot_hi(n0, dot_hi(pq0, n0, 1, 0) + dot_hi(g02, m1, 1, 0), 0, 0) + dot_hi(
         m1, dot_hi(g02, n0, 0, 0), 0, 0
     )
+    z_stage(1, zs)
+    next(red_d)
     found = []
 
     def finish():
+        residual = combine(m0, probes) + combine(m1, basis)
+        direction = residual + combine(beta, probes)
+        xsol = combine(alpha, probes)
+        partial = combine(n0, image) + combine(m1, own)
         g12 = unfold(next(red_d))
-        found.append(solve(known + dot_hi(m1, dot_hi(g12, m1, 1, 0), 0, 0), rr1))
+        gamma = solve(known + dot_hi(m1, dot_hi(g12, m1, 1, 0), 0, 0), rr1)
+        found.extend((residual, direction, xsol, partial, gamma))
 
     last = plane_stage2(1, mid, {3: finish})
     drain(1)
-    gamma = found[0]
+    residual, direction, xsol, partial, gamma = found
     deep = z_end(1, zs)
     deep = deep + plane_end(1, last)
-    image2 = partial + combine(m1, own + unpack(deep))
+    image2 = partial + combine(m1, unpack(deep))
     sol_ref[...] = xsol + combine(gamma, direction)
     res_ref[...] = residual - combine(gamma, image2)
 

time: 89.7 us -> 87.9 us (0.980)
  Pallas kernels: 88.2 us -> 86.2 us
    pallas_call x1, Pallas kernels: 86.5 us -> 84.5 us  [body(): pl.pallas_call(kernel, out_shape=(wide, wide), in_specs=[smem, smem, smem...]
where the time goes in v5:
time: 87.9 us; the launch traced here: 87.5 us
  Pallas kernels  86.2 us (98%)
  between operations  1.29 us (1%)
    pallas_call x1, Pallas kernels, body(): pl.pallas_call(kernel, out_shape=(wide, wide), in_specs=[smem, smem, smem...  84.5 us

profile of v5, /device:TPU:8, one launch (start us, length us, event | category | flops | bytes accessed | tf_op | source)
XLA Modules:
  0.0 87.5 jit_solution(4751469224922758958)
XLA Ops:
  1.3 84.5 %block_cg.1 = (f32[64,576]{1,0:T(8,128)}, f32[64,576]{1,0:T(8,128)}) custom-call(s32[1,1,16]{2,1,0:T(1,128)} %rows_ref.1, s32[1,1,16]{2,1,0:T(1,128)} %cols_ref.1, s32[1,1]{1,0:T(1,128)S(6)} %copy.8.counts_ref, bf16[1,1,16,576,576]{4,3,2,1,0:T(8,128)(2,1)} %tiles_ref.1, bf16[1,576,576]{2,1,0:T(8,128)(2,1)} %diag_ref.1, f32[1,64,576]{2,1,0:T(8,128)} %probes_ref.1), custom_call_target="tpu_custom_call" | custom-call | tf_op jit(solution)/shard_map/block_cg/pallas_call | solution.py:557
  85.8 1.7 %close.1 = (f32[1,64,576]{2,1,0:T(8,128)}, f32[1,64,576]{2,1,0:T(8,128)}) custom-call(f32[64,576]{1,0:T(8,128)} %get-tuple-element.4.sol_ref, f32[64,576]{1,0:T(8,128)} %get-tuple-element.5.res_ref), custom_call_target="tpu_custom_call" | custom-call | tf_op jit(solution)/shard_map/close/pallas_call | solution.py:605

commit v6 on v5

--- a/solution.py
+++ b/solution.py
@@ -447,12 +447,11 @@
     next(red_a)
     gather_end_plane(0, state)
     mid = {}
-    cross = mirror_products(0, 0, 8, jnp.zeros((Q, Q), jnp.float32))
+    cross = mirror_products(0, 0, 12, jnp.zeros((Q, Q), jnp.float32))
     mid[2] = plane_stage(0, across, 2)
-    cross = mirror_products(0, 8, 12, cross)
-    mid[1] = plane_stage(0, across, 1)
     cross = mirror_products(0, 12, 16, cross)
     zs = z_begin(0)
+    mid[1] = plane_stage(0, across, 1)
     mid[3] = plane_stage(0, across, 3)
     mid[0] = plane_stage(0, across, 0)
     cross = late_cross(0, cross)
@@ -493,15 +492,14 @@
     next(red_c)
     gather_end_plane(1, state)
     mid = {}
-    cross = mirror_products(1, 0, 8, jnp.zeros((Q, Q), jnp.float32))
+    cross = mirror_products(1, 0, 12, jnp.zeros((Q, Q), jnp.float32))
     mid[2] = plane_stage(1, across, 2)
-    cross = mirror_products(1, 8, 12, cross)
-    mid[1] = plane_stage(1, across, 1)
     cross = mirror_products(1, 12, 16, cross)
     cross = cross + cross.T
     zs = z_begin(1)
     red_d = reduce_steps(ar_d, ar_dr, fold(gram(basis, own) + cross))
     next(red_d)
+    mid[1] = plane_stage(1, across, 1)
     mid[3] = plane_stage(1, across, 3)
     mid[0] = plane_stage(1, across, 0)
     next(red_d)

time: 87.9 us -> 87.7 us (level)
  no operation moved by 1% of the time
where the time goes in v6:
time: 87.7 us; the launch traced here: 87.6 us
  Pallas kernels  86.3 us (98%)
  between operations  1.29 us (1%)
    pallas_call x1, Pallas kernels, body(): pl.pallas_call(kernel, out_shape=(wide, wide), in_specs=[smem, smem, smem...  84.6 us

profile of v6, /device:TPU:8, one launch (start us, length us, event | category | flops | bytes accessed | tf_op | source)
XLA Modules:
  0.0 87.6 jit_solution(15034631433811556640)
XLA Ops:
  1.3 84.6 %block_cg.1 = (f32[64,576]{1,0:T(8,128)}, f32[64,576]{1,0:T(8,128)}) custom-call(s32[1,1,16]{2,1,0:T(1,128)} %rows_ref.1, s32[1,1,16]{2,1,0:T(1,128)} %cols_ref.1, s32[1,1]{1,0:T(1,128)S(6)} %copy.8.counts_ref, bf16[1,1,16,576,576]{4,3,2,1,0:T(8,128)(2,1)} %tiles_ref.1, bf16[1,576,576]{2,1,0:T(8,128)(2,1)} %diag_ref.1, f32[1,64,576]{2,1,0:T(8,128)} %probes_ref.1), custom_call_target="tpu_custom_call" | custom-call | tf_op jit(solution)/shard_map/block_cg/pallas_call | solution.py:555
  85.8 1.7 %close.1 = (f32[1,64,576]{2,1,0:T(8,128)}, f32[1,64,576]{2,1,0:T(8,128)}) custom-call(f32[64,576]{1,0:T(8,128)} %get-tuple-element.4.sol_ref, f32[64,576]{1,0:T(8,128)} %get-tuple-element.5.res_ref), custom_call_target="tpu_custom_call" | custom-call | tf_op jit(solution)/shard_map/close/pallas_call | solution.py:603
